TPU v7x, 32 devices: a whole 2x2x4 slice. The times are simulated.
32 devices in a mesh: dp: 16 (over z, y, x), mp: 2 (over core).
Axes of the slice: x: 2, y: 2, z: 4, core: 2. Of those that a mesh axis runs over, the one named last changes fastest.
Arguments:
- tokens: bfloat16 [32, 512, 768], P('dp', 'mp'), may hold values from -6 to 6
- lengths: int32 [32, 16], P('dp'), may hold values from 0 to 512, as said below
- cotangent: bfloat16 [32, 512, 768], P('dp', 'mp'), may hold values from -6 to 6
- w_query: bfloat16 [2, 768, 768], P(None, None, 'mp'), may hold values from -0.21875 to 0.21875
- b_query: bfloat16 [2, 768], P(None, 'mp'), may hold values from -3 to 3
- w_key: bfloat16 [2, 768, 768], P(None, None, 'mp'), may hold values from -0.21875 to 0.21875
- w_value: bfloat16 [2, 768, 768], P(None, None, 'mp'), may hold values from -0.21875 to 0.21875
- b_value: bfloat16 [2, 768], P(None, 'mp'), may hold values from -3 to 3
- w_out: bfloat16 [2, 768, 768], P(None, None, 'mp'), may hold values from -1.75 to 1.75
- b_out: bfloat16 [2, 768], replicated, may hold values from -3 to 3
- first_gain: bfloat16 [2, 768], replicated, may hold values from 0.099609375 to 1.8984375
- first_shift: bfloat16 [2, 768], replicated, may hold values from -3 to 3
- w_up: bfloat16 [2, 768, 3072], P(None, None, 'mp'), may hold values from -0.21875 to 0.21875
- b_up: bfloat16 [2, 3072], P(None, 'mp'), may hold values from -3 to 3
- w_down: bfloat16 [2, 768, 3072], P(None, None, 'mp'), may hold values from -0.109375 to 0.109375
- b_down: bfloat16 [2, 768], replicated, may hold values from -3 to 3
- second_gain: bfloat16 [2, 768], replicated, may hold values from 0.099609375 to 1.8984375
- second_shift: bfloat16 [2, 768], replicated, may hold values from -3 to 3
Outputs:
- encoded: bfloat16 [32, 512, 768], P('dp', 'mp')
- token_grad: float32 [32, 512, 768], P('dp', 'mp')
- grad_w_query: float32 [2, 768, 768], P(None, 'dp', 'mp')
- grad_b_query: float32 [2, 768], P(None, 'mp')
- grad_w_key: float32 [2, 768, 768], P(None, 'dp', 'mp')
- grad_w_value: float32 [2, 768, 768], P(None, 'dp', 'mp')
- grad_b_value: float32 [2, 768], P(None, 'mp')
- grad_w_out: float32 [2, 768, 768], P(None, 'dp', 'mp')
- grad_b_out: float32 [2, 768], replicated
- grad_first_gain: float32 [2, 768], replicated
- grad_first_shift: float32 [2, 768], replicated
- grad_w_up: float32 [2, 768, 3072], P(None, 'dp', 'mp')
- grad_b_up: float32 [2, 3072], P(None, 'mp')
- grad_w_down: float32 [2, 768, 3072], P(None, 'dp', 'mp')
- grad_b_down: float32 [2, 768], replicated
- grad_second_gain: float32 [2, 768], replicated
- grad_second_shift: float32 [2, 768], replicated
Inputs may be any that keep to these rules, and one draw needn't show every extreme that they name: In each row either entries 1 to 15 are 0 and entry 0 is a passage's length, at least 64, or all 16 entries are lengths of queries, each at least 1 and at most 32. Some row holds a passage of 512 slots and some query fills its 32 slots.
All inputs are finite; a program needn't handle non-finite values.
Results may differ from a plain program's by a relative error of at most 0.04.
Values may be sent and summed in bfloat16 or wider, within the bound.
No kernel may reach another device: no remote copies, remote signals or barrier semaphores. Data moves between devices by JAX's collectives and lax.ppermute only.
A program may use at most 192 MiB of HBM per device.

v0:
```python
import jax
import jax.numpy as jnp
from jax import lax
from jax.sharding import PartitionSpec as P

DH = 64
SLOTS = 512
QSLOT = 32
SEGS = 16


def visible_mask(lengths):
    slot_index = jnp.arange(SLOTS, dtype=jnp.int32)
    is_query = lengths[:, 1] > 0
    segment_width = jnp.where(is_query, QSLOT, SLOTS).astype(jnp.int32)[:, None]
    segment = slot_index[None, :] // segment_width
    inside = slot_index[None, :] - segment * segment_width
    onehot = segment[:, :, None] == jnp.arange(SEGS, dtype=jnp.int32)[None, None, :]
    segment_length = jnp.sum(jnp.where(onehot, lengths[:, None, :], 0), axis=2)
    live_keys = inside < segment_length
    same_segment = segment[:, :, None] == segment[:, None, :]
    return same_segment & live_keys[:, None, :]


def layer_norm(residual, norm_gain, norm_shift):
    average = jnp.mean(residual, axis=-1, keepdims=True)
    centred = residual - average
    variance = jnp.mean(centred * centred, axis=-1, keepdims=True)
    return centred * lax.rsqrt(variance + 1e-12) * norm_gain + norm_shift


def gelu_exact(argument):
    return 0.5 * argument * (1.0 + jax.scipy.special.erf(argument * 0.7071067811865476))


def project(left, right):
    return jnp.einsum("rsd,de->rse", left, right, preferred_element_type=jnp.float32)


def attend(row_data):
    row_queries, row_keys, row_values, visible = row_data
    head_count = row_queries.shape[1] // DH
    query_heads = row_queries.reshape(SLOTS, head_count, DH)
    key_heads = row_keys.reshape(SLOTS, head_count, DH)
    value_heads = row_values.reshape(SLOTS, head_count, DH)
    scores = jnp.einsum(
        "shd,thd->hst", query_heads, key_heads, preferred_element_type=jnp.float32
    ) * DH ** (-0.5)
    scores = jnp.where(visible[None], scores, -1000000000.0)
    row_peak = jnp.max(scores, axis=2, keepdims=True)
    exponent = jnp.exp(scores - row_peak)
    summed = jnp.sum(exponent, axis=2, keepdims=True)
    weights_low = (exponent / summed).astype(jnp.bfloat16)
    context = jnp.einsum(
        "hst,thd->shd", weights_low, value_heads, preferred_element_type=jnp.float32
    )
    return (
        context.reshape(SLOTS, head_count * DH).astype(jnp.bfloat16),
        (row_peak + jnp.log(summed))[:, :, 0],
    )


def attend_back(row_data):
    row_queries, row_keys, row_values, visible, log_total, context_grad = row_data
    head_count = row_queries.shape[1] // DH
    width = head_count * DH
    query_heads = row_queries.reshape(SLOTS, head_count, DH)
    key_heads = row_keys.reshape(SLOTS, head_count, DH)
    value_heads = row_values.reshape(SLOTS, head_count, DH)
    grad_heads = context_grad.reshape(SLOTS, head_count, DH)
    scores = jnp.einsum(
        "shd,thd->hst", query_heads, key_heads, preferred_element_type=jnp.float32
    ) * DH ** (-0.5)
    probabilities = jnp.where(visible[None], jnp.exp(scores - log_total[:, :, None]), 0.0)
    weights_low = probabilities.astype(jnp.bfloat16)
    value_grad = jnp.einsum(
        "hst,shd->thd", weights_low, grad_heads, preferred_element_type=jnp.float32
    )
    weight_grad = jnp.einsum(
        "shd,thd->hst", grad_heads, value_heads, preferred_element_type=jnp.float32
    )
    score_grad = (
        probabilities * (weight_grad - jnp.sum(probabilities * weight_grad, axis=2, keepdims=True))
    ).astype(jnp.bfloat16)
    query_grad = jnp.einsum(
        "hst,thd->shd", score_grad, key_heads, preferred_element_type=jnp.float32
    ) * DH ** (-0.5)
    key_grad = jnp.einsum(
        "hst,shd->thd", score_grad, query_heads, preferred_element_type=jnp.float32
    ) * DH ** (-0.5)
    return (
        query_grad.reshape(SLOTS, width).astype(jnp.bfloat16),
        key_grad.reshape(SLOTS, width).astype(jnp.bfloat16),
        value_grad.reshape(SLOTS, width).astype(jnp.bfloat16),
    )


def forward_layer(block_in, weights, visibility):
    (
        w_query,
        b_query,
        w_key,
        w_value,
        b_value,
        w_out,
        b_out,
        first_gain,
        first_shift,
        w_up,
        b_up,
        w_down,
        b_down,
        second_gain,
        second_shift,
    ) = weights
    gathered = lax.all_gather(block_in, "mp", axis=1, tiled=True)
    queries = (project(gathered, w_query) + b_query.astype(jnp.float32)).astype(jnp.bfloat16)
    keys_all = project(gathered, w_key).astype(jnp.bfloat16)
    values_all = (project(gathered, w_value) + b_value.astype(jnp.float32)).astype(jnp.bfloat16)
    context, log_total = lax.map(attend, (queries, keys_all, values_all, visibility))
    partial_out = jnp.einsum("rsc,dc->rsd", context, w_out, preferred_element_type=jnp.float32)
    attended = lax.psum_scatter(
        partial_out.astype(jnp.bfloat16), "mp", scatter_dimension=1, tiled=True
    ).astype(jnp.float32) + b_out.astype(jnp.float32)
    first_resid = block_in.astype(jnp.float32) + attended
    normed = layer_norm(
        first_resid, first_gain.astype(jnp.float32), first_shift.astype(jnp.float32)
    )
    gathered_normed = lax.all_gather(normed.astype(jnp.bfloat16), "mp", axis=1, tiled=True)
    upward = project(gathered_normed, w_up) + b_up.astype(jnp.float32)
    activated = gelu_exact(upward).astype(jnp.bfloat16)
    partial_down = jnp.einsum("rsf,df->rsd", activated, w_down, preferred_element_type=jnp.float32)
    downward = lax.psum_scatter(
        partial_down.astype(jnp.bfloat16), "mp", scatter_dimension=1, tiled=True
    ).astype(jnp.float32) + b_down.astype(jnp.float32)
    second_resid = normed + downward
    output = layer_norm(
        second_resid, second_gain.astype(jnp.float32), second_shift.astype(jnp.float32)
    )
    kept_state = (
        gathered,
        queries,
        keys_all,
        values_all,
        context,
        log_total,
        first_resid,
        gathered_normed,
        upward,
        activated,
        second_resid,
    )
    return (output, kept_state)


def backward_layer(weights, visibility, kept_state, grad_out):
    (
        w_query,
        b_query,
        w_key,
        w_value,
        b_value,
        w_out,
        b_out,
        first_gain,
        first_shift,
        w_up,
        b_up,
        w_down,
        b_down,
        second_gain,
        second_shift,
    ) = weights
    (
        gathered,
        queries,
        keys_all,
        values_all,
        context,
        log_total,
        first_resid,
        gathered_normed,
        upward,
        activated,
        second_resid,
    ) = kept_state
    unused, pull_second = jax.vjp(
        layer_norm, second_resid, second_gain.astype(jnp.float32), second_shift.astype(jnp.float32)
    )
    grad_second, grad_second_gain, grad_second_shift = pull_second(grad_out)
    down_grad = grad_second.astype(jnp.bfloat16)
    grad_b_down = jnp.sum(down_grad, axis=(0, 1), dtype=jnp.float32)
    gathered_down = lax.all_gather(down_grad, "mp", axis=1, tiled=True)
    grad_w_down = jnp.einsum(
        "rsd,rsf->df", gathered_down, activated, preferred_element_type=jnp.float32
    )
    act_grad = jnp.einsum("rsd,df->rsf", gathered_down, w_down, preferred_element_type=jnp.float32)
    unused, pull_gelu = jax.vjp(gelu_exact, upward)
    up_grad = pull_gelu(act_grad)[0].astype(jnp.bfloat16)
    grad_b_up = jnp.sum(up_grad, axis=(0, 1), dtype=jnp.float32)
    grad_w_up = jnp.einsum(
        "rsd,rsf->df", gathered_normed, up_grad, preferred_element_type=jnp.float32
    )
    partial_normed = jnp.einsum("rsf,df->rsd", up_grad, w_up, preferred_element_type=jnp.float32)
    normed_grad = grad_second + lax.psum_scatter(
        partial_normed.astype(jnp.bfloat16), "mp", scatter_dimension=1, tiled=True
    ).astype(jnp.float32)
    unused, pull_first = jax.vjp(
        layer_norm, first_resid, first_gain.astype(jnp.float32), first_shift.astype(jnp.float32)
    )
    grad_first, grad_first_gain, grad_first_shift = pull_first(normed_grad)
    out_grad = grad_first.astype(jnp.bfloat16)
    grad_b_out = jnp.sum(out_grad, axis=(0, 1), dtype=jnp.float32)
    gathered_out = lax.all_gather(out_grad, "mp", axis=1, tiled=True)
    grad_w_out = jnp.einsum(
        "rsd,rsc->dc", gathered_out, context, preferred_element_type=jnp.float32
    )
    context_grad = jnp.einsum(
        "rsd,dc->rsc", gathered_out, w_out, preferred_element_type=jnp.float32
    ).astype(jnp.bfloat16)
    query_grad, key_grad, value_grad = lax.map(
        attend_back, (queries, keys_all, values_all, visibility, log_total, context_grad)
    )
    grad_b_query = jnp.sum(query_grad, axis=(0, 1), dtype=jnp.float32)
    grad_b_value = jnp.sum(value_grad, axis=(0, 1), dtype=jnp.float32)
    grad_w_query = jnp.einsum(
        "rsd,rse->de", gathered, query_grad, preferred_element_type=jnp.float32
    )
    grad_w_key = jnp.einsum("rsd,rse->de", gathered, key_grad, preferred_element_type=jnp.float32)
    grad_w_value = jnp.einsum(
        "rsd,rse->de", gathered, value_grad, preferred_element_type=jnp.float32
    )
    partial_in = jnp.einsum("rse,de->rsd", query_grad, w_query, preferred_element_type=jnp.float32)
    partial_in = partial_in + jnp.einsum(
        "rse,de->rsd", key_grad, w_key, preferred_element_type=jnp.float32
    )
    partial_in = partial_in + jnp.einsum(
        "rse,de->rsd", value_grad, w_value, preferred_element_type=jnp.float32
    )
    block_grad = grad_first + lax.psum_scatter(
        partial_in.astype(jnp.bfloat16), "mp", scatter_dimension=1, tiled=True
    ).astype(jnp.float32)
    gradients = (
        grad_w_query,
        grad_b_query,
        grad_w_key,
        grad_w_value,
        grad_b_value,
        grad_w_out,
        grad_b_out,
        grad_first_gain,
        grad_first_shift,
        grad_w_up,
        grad_b_up,
        grad_w_down,
        grad_b_down,
        grad_second_gain,
        grad_second_shift,
    )
    return (block_grad, gradients)


def shards(
    tokens,
    lengths,
    cotangent,
    w_query,
    b_query,
    w_key,
    w_value,
    b_value,
    w_out,
    b_out,
    first_gain,
    first_shift,
    w_up,
    b_up,
    w_down,
    b_down,
    second_gain,
    second_shift,
):
    params = (
        w_query,
        b_query,
        w_key,
        w_value,
        b_value,
        w_out,
        b_out,
        first_gain,
        first_shift,
        w_up,
        b_up,
        w_down,
        b_down,
        second_gain,
        second_shift,
    )
    visibility = visible_mask(lengths)
    layer_count = w_query.shape[0]
    block_inputs = []
    kept_states = []
    hidden = tokens
    for layer_index in range(layer_count):
        weights = tuple((member[layer_index] for member in params))
        block_inputs.append(hidden)
        output, kept_state = forward_layer(hidden, weights, visibility)
        kept_states.append(kept_state)
        hidden = output.astype(jnp.bfloat16)
    grad_hidden = cotangent.astype(jnp.float32)
    layer_grads = [None] * layer_count
    for layer_index in reversed(range(layer_count)):
        weights = tuple((member[layer_index] for member in params))
        kept_state = forward_layer(block_inputs[layer_index], weights, visibility)[1]
        grad_hidden, gradients = backward_layer(weights, visibility, kept_state, grad_hidden)
        layer_grads[layer_index] = gradients
    stacked = [
        jnp.stack([layer_grads[layer_index][member_index] for layer_index in range(layer_count)])
        for member_index in range(15)
    ]
    matrices = (
        lax.psum_scatter(stacked[0], "dp", scatter_dimension=1, tiled=True),
        lax.psum_scatter(stacked[2], "dp", scatter_dimension=1, tiled=True),
        lax.psum_scatter(stacked[3], "dp", scatter_dimension=1, tiled=True),
        lax.psum_scatter(stacked[5], "dp", scatter_dimension=1, tiled=True),
        lax.psum_scatter(stacked[9], "dp", scatter_dimension=1, tiled=True),
        lax.psum_scatter(stacked[11], "dp", scatter_dimension=1, tiled=True),
    )
    columns = lax.psum((stacked[1], stacked[4], stacked[10]), "dp")
    rows_summed = lax.psum(
        (stacked[6], stacked[7], stacked[8], stacked[12], stacked[13], stacked[14]), ("dp", "mp")
    )
    return (
        hidden,
        grad_hidden,
        matrices[0],
        columns[0],
        matrices[1],
        matrices[2],
        columns[1],
        matrices[3],
        rows_summed[0],
        rows_summed[1],
        rows_summed[2],
        matrices[4],
        columns[2],
        matrices[5],
        rows_summed[3],
        rows_summed[4],
        rows_summed[5],
    )


def solution(mesh):
    placed = (
        P("dp", "mp", None),
        P("dp", None),
        P("dp", "mp", None),
        P(None, None, "mp"),
        P(None, "mp"),
        P(None, None, "mp"),
        P(None, None, "mp"),
        P(None, "mp"),
        P(None, None, "mp"),
        P(),
        P(),
        P(),
        P(None, None, "mp"),
        P(None, "mp"),
        P(None, None, "mp"),
        P(),
        P(),
        P(),
    )
    return jax.shard_map(
        shards,
        mesh=mesh,
        in_specs=placed,
        out_specs=(
            P("dp", "mp", None),
            P("dp", "mp", None),
            P(None, "dp", "mp"),
            P(None, "mp"),
            P(None, "dp", "mp"),
            P(None, "dp", "mp"),
            P(None, "mp"),
            P(None, "dp", "mp"),
            P(),
            P(),
            P(),
            P(None, "dp", "mp"),
            P(None, "mp"),
            P(None, "dp", "mp"),
            P(),
            P(),
            P(),
        ),
        check_vma=False,
    )
```

profile of v0, /device:TPU:0, one launch (start us, length us, event | category | flops | bytes accessed | tf_op | source)
XLA Modules:
  0.0 1288.8 jit_solution(6457793700679230937)
XLA Ops:
  13.4 8.7 all-gather.11.cloned.1.call-done
  22.1 3.4 add_convert_fusion.9
  31.7 3.4 convolution_convert_fusion.7
  37.4 24.5 %while.72 = (s32[]{:T(128)}, bf16[2,512,384]{1,2,0:T(8,128)(2,1)}, bf16[2,512,384]{1,2,0:T(8,128)(2,1)S(1)}, pred[2,512,512]{1,2,0:T(8,128)(4,1)S(1)}, bf16[2,51...) while((s32[]{:T(128)}, bf16[2,512,384]{1,2,0:T(8,128)(2,1)}, ...), condition=%wide.region_4.5_spmd, body=%wide.region_1.4_spmd.sunk | while | flops 412287488 | bytes 24404124 | solution.py:120
  38.4 6.8 fusion.329
  45.2 3.5 fusion.330
  50.7 6.8 fusion.329
  57.5 3.5 fusion.330
  62.0 3.5 convolution_convert_fusion.3
  66.7 11.2 while.76
  78.9 4.1 convolution_convert_fusion
  85.8 7.5 reduce-scatter.32.cloned.1.call-done
  97.4 10.5 all-gather.13.cloned.1.call-done
  107.9 9.2 fusion.93
  118.4 9.1 reduce-scatter.18.cloned.1.call-done
  132.3 11.1 all-gather.25.cloned.1.call-done
  143.4 6.6 multiply_convert_fusion.2
  151.6 5.4 fusion.96
  158.4 9.1 reduce-scatter.34.cloned.1.call-done
  167.5 4.9 fusion.183
  172.5 11.1 all-gather.15.cloned.1.call-done
  183.6 3.4 add_convert_fusion.5
  188.5 3.3 add_convert_fusion.6
  197.8 22.5 %while.73 = (s32[]{:T(128)}, bf16[2,512,384]{1,2,0:T(8,128)(2,1)}, bf16[2,512,384]{1,2,0:T(8,128)(2,1)S(1)}, pred[2,512,512]{1,2,0:T(8,128)(4,1)S(1)}, bf16[2,51...) while((s32[]{:T(128)}, bf16[2,512,384]{1,2,0:T(8,128)(2,1)}, ...), condition=%wide.region_14.15_spmd, body=%wide.region_11.14_spmd.sunk | while | flops 412287488 | bytes 24404124 | solution.py:120
  199.0 5.7 fusion.334
  204.6 3.5 fusion.335
  210.2 5.7 fusion.334
  215.9 3.5 fusion.335
  220.4 3.5 convolution_convert_fusion.2
  224.2 11.4 while.74
  236.5 3.6 convolution_convert_fusion.1
  241.8 8.7 reduce-scatter.24.cloned.1.call-done
  254.0 11.1 all-gather.17.cloned.1.call-done
  265.1 9.2 fusion.102
  274.6 10.1 reduce-scatter.22.cloned.1.call-done
  288.8 11.1 all-gather.19.cloned.1.call-done
  299.9 6.6 multiply_convert_fusion.3
  308.1 5.5 fusion.105
  313.6 10.3 reduce-scatter.26.cloned.1.call-done
  331.7 11.1 all-gather.21.cloned.1.call-done
  342.9 8.0 convert_reduce_fusion
  352.5 5.4 fusion.99
  358.1 10.3 reduce-scatter.28.cloned.1.call-done
  368.4 4.2 multiply_reduce_fusion.3
  376.9 10.7 all-gather.23.cloned.1.call-done
  392.9 30.1 %while.75 = (s32[]{:T(128)}, bf16[2,512,384]{1,2,0:T(8,128)(2,1)}, bf16[2,512,384]{1,2,0:T(8,128)(2,1)}, bf16[2,512,384]{1,2,0:T(8,128)(2,1)}, bf16[2,512,384]{1...) while((s32[]{:T(128)}, bf16[2,512,384]{1,2,0:T(8,128)(2,1)}, ...), condition=%wide.region_38.39_spmd, body=%wide.region_36.38_spmd.sunk | while | flops 1031205888 | bytes 93606456 | solution.py:221
  431.1 8.7 reduce-scatter.30.cloned.1.call-done
  446.9 11.1 all-gather.27.cloned.1.call-done
  458.0 8.2 convert_reduce_fusion.1
  467.9 3.8 fusion.90
  471.7 10.3 reduce-scatter.36.cloned.1.call-done
  488.4 10.9 all-gather.29.cloned.1.call-done
  504.6 32.2 %while.77 = (s32[]{:T(128)}, bf16[2,512,384]{1,2,0:T(8,128)(2,1)}, bf16[2,512,384]{1,2,0:T(8,128)(2,1)}, bf16[2,512,384]{1,2,0:T(8,128)(2,1)}, bf16[2,512,384]{1...) while((s32[]{:T(128)}, bf16[2,512,384]{1,2,0:T(8,128)(2,1)}, ...), condition=%wide.region_57.58_spmd, body=%wide.region_55.57_spmd.sunk | while | flops 1031205888 | bytes 87118264 | solution.py:221
  573.8 4.7 convolution_bitcast_fusion
  581.2 4.5 pad_maximum_fusion.1
  585.9 5.2 convolution_bitcast_fusion.2
  593.8 4.5 pad_maximum_fusion
  600.5 3.9 add_convert_fusion.4
  605.3 43.8 %all-reduce.3 = (f32[2,768]{1,0:T(2,128)}, f32[2,768]{1,0:T(2,128)}, f32[2,768]{1,0:T(2,128)}, f32[2,768]{1,0:T(2,128)}, f32[2,768]{1,0:T(2,128)}, /*index=5*/f32[2,768]{1,0:T(2,128)}) all-reduce(f32[2,768]{1,0:T(2,128)S(1)} %pad_maximum_fusion.7, f32[2,768]{1,0:T(2,128)S(1)} %pad_maximum_fusion.8, ...), channel_id=1, replica_groups=mesh['dp'=16,'mp'=2] {'dp','mp'}, use_global_device_ids=true, to_apply=%region_71.72 | all-reduce | flops 9216 | bytes 73728 | tf_op jit(solution)/shard_map/psum | solution.py:331
  649.5 76.7 %all-reduce.4 = (f32[2,384]{1,0:T(2,128)}, f32[2,384]{1,0:T(2,128)}, f32[2,1536]{1,0:T(2,128)}) all-reduce(f32[2,384]{1,0:T(2,128)S(1)} %pad_maximum_fusion.13, f32[2,384]{1,0:T(2,128)S(1)} %pad_maximum_fusion.14, f32[2,1536]{1,0:T(2,128)S(1)} %pad_maximum_fusion.6), channel_id=1, replica_groups=mesh['dp'=16,'mp'=2] {'dp'}, use_global_device_ids=true, to_apply=%region_62.63 | all-reduce | flops 4608 | bytes 36864 | tf_op jit(solution)/shard_map/psum | solution.py:330
  728.7 68.2 %all-reduce.8.cloned.1.call-done = (f32[2,768,384]{2,0,1:T(2,128)}, f32[2,768,384]{2,0,1:T(2,128)}, f32[2,768,384]{2,0,1:T(2,128)}) async-done(((f32[2,768,384]{2,0,1:T(2,128)}, f32[2,768,384]{2,0,1:T(2,128)}, f32[2,768,384]{2,0,1:T(2,128)}), (f32[2,768,384]{2,0,1:T(2,128)}, f32[2,768,384]{2,0,1:T(2,128)}, f32[2,768,384]{2,0,1:T(2,128)})) %all-reduce.8.cloned.1.call-update) | async-done | bytes 7077904
  801.8 127.2 %reduce-scatter.40.cloned.1.call-done = f32[2,48,384]{2,1,0:T(8,128)} async-done(((f32[2,768,384]{2,1,0:T(8,128)}), f32[2,48,384]{2,1,0:T(8,128)}) %reduce-scatter.40.cloned.1.call-update) | async-done | bytes 147472 | tf_op jit(solution)/shard_map/reduce_scatter | solution.py:326
  929.0 177.2 %reduce-scatter.44.cloned.1.call-done = f32[2,48,1536]{2,1,0:T(8,128)} async-done(((f32[2,768,1536]{2,1,0:T(8,128)}), f32[2,48,1536]{2,1,0:T(8,128)}) %reduce-scatter.44.cloned.1.call-update) | async-done | bytes 589840 | tf_op jit(solution)/shard_map/reduce_scatter | solution.py:328
  1106.2 175.9 %reduce-scatter.42.cloned.1.call-done = f32[2,48,1536]{2,1,0:T(8,128)} async-done(((f32[2,768,1536]{2,1,0:T(8,128)}), f32[2,48,1536]{2,1,0:T(8,128)}) %reduce-scatter.42.cloned.1.call-update) | async-done | bytes 589840 | tf_op jit(solution)/shard_map/reduce_scatter | solution.py:327
  (672 shorter events, 243.8 us)
Async XLA Ops:
  7.2 14.9 %all-gather.11.cloned.1.call-start = ((), (), s32[]{:S(2)}) async-start(), calls=%async_computation.15 | async-start | bytes 2359296 | tf_op jit(solution)/shard_map/all_gather | solution.py:116
  7.9 76.4 %reduce-scatter.16.cloned.1.call-start = ((), (), s32[]{:S(2)}) async-start(), calls=%async_computation.16 | async-start | bytes 2359296 | tf_op jit(solution)/shard_map/reduce_scatter | solution.py:122
  65.4 27.9 %reduce-scatter.32.cloned.1.call-start = ((), (), s32[]{:S(2)}) async-start(), calls=%async_computation.30 | async-start | bytes 2359296 | tf_op jit(solution)/shard_map/reduce_scatter | solution.py:122
  78.8 4.8 copy-start.130
  78.8 4.8 copy-start.131
  78.8 5.4 copy-start.2
  83.0 24.9 %all-gather.13.cloned.1.call-start = ((), (), s32[]{:S(2)}) async-start(), calls=%async_computation.17 | async-start | bytes 2359296 | tf_op jit(solution)/shard_map/all_gather | solution.py:129
  83.6 83.8 %copy-start.86 = (f32[768]{0:T(1024)}, f32[768]{0:T(1024)S(1)}, u32[]{:S(2)}) copy-start(f32[768]{0:T(1024)S(1)} %get-tuple-element.490) | copy-start | bytes 9220
  84.3 83.2 %copy-start.94 = (f32[768]{0:T(1024)}, f32[768]{0:T(1024)S(1)}, u32[]{:S(2)}) copy-start(f32[768]{0:T(1024)S(1)} %get-tuple-element.664) | copy-start | bytes 9220
  84.3 9.0 copy-start.14
  96.7 30.8 %reduce-scatter.18.cloned.1.call-start = ((), (), s32[]{:S(2)}) async-start(), calls=%async_computation.18 | async-start | bytes 2359296 | tf_op jit(solution)/shard_map/reduce_scatter | solution.py:133
  97.4 46.0 %copy-start.137 = (f32[1536]{0:T(1024)}, f32[1536]{0:T(1024)S(1)}, u32[]{:S(2)}) copy-start(f32[1536]{0:T(1024)S(1)} %get-tuple-element.488) | copy-start | bytes 18436
  117.1 12.4 copy-start.12
  117.1 26.3 %all-gather.25.cloned.1.call-start = ((), (), s32[]{:S(2)}) async-start(), calls=%async_computation.31 | async-start | bytes 2359296 | tf_op jit(solution)/shard_map/all_gather | solution.py:129
  118.4 49.1 %copy-start.102 = (f32[2,256]{1,0:T(2,128)}, f32[2,256]{1,0:T(2,128)S(1)}, u32[]{:S(2)}) copy-start(f32[2,256]{1,0:T(2,128)S(1)} %broadcast_multiply_fusion.1) | copy-start | bytes 6148
  130.9 36.6 %copy-start.110 = (f32[2,256]{1,0:T(2,128)}, f32[2,256]{1,0:T(2,128)S(1)}, u32[]{:S(2)}) copy-start(f32[2,256]{1,0:T(2,128)S(1)} %fusion.166) | copy-start | bytes 6148
  132.2 35.2 %reduce-scatter.34.cloned.1.call-start = ((), (), s32[]{:S(2)}) async-start(), calls=%async_computation.32 | async-start | bytes 2359296 | tf_op jit(solution)/shard_map/reduce_scatter | solution.py:133
  157.1 26.5 %all-gather.15.cloned.1.call-start = ((), (), s32[]{:S(2)}) async-start(), calls=%async_computation.19 | async-start | bytes 2359296 | tf_op jit(solution)/shard_map/all_gather | solution.py:116
  158.4 14.0 %copy-start.108 = (f32[768]{0:T(1024)}, f32[768]{0:T(1024)S(1)}, u32[]{:S(2)}) copy-start(f32[768]{0:T(1024)S(1)} %get-tuple-element.667) | copy-start | bytes 9220
  167.5 16.1 %copy-start.143 = (f32[384]{0:T(512)S(1)}, f32[384]{0:T(512)}, u32[]{:S(2)}) copy-start(f32[384]{0:T(512)} %get-tuple-element.501) | copy-start | bytes 4612
  172.4 67.8 %reduce-scatter.20.cloned.1.call-start = ((), (), s32[]{:S(2)}) async-start(), calls=%async_computation.20 | async-start | bytes 2359296 | tf_op jit(solution)/shard_map/reduce_scatter | solution.py:122
  223.9 26.6 %reduce-scatter.24.cloned.1.call-start = ((), (), s32[]{:S(2)}) async-start(), calls=%async_computation.23 | async-start | bytes 2359296 | tf_op jit(solution)/shard_map/reduce_scatter | solution.py:122
  240.1 25.0 %all-gather.17.cloned.1.call-start = ((), (), s32[]{:S(2)}) async-start(), calls=%async_computation.21 | async-start | bytes 2359296 | tf_op jit(solution)/shard_map/all_gather | solution.py:129
  240.2 10.3 copy-start.16
  241.7 10.8 copy-start.96
  241.7 10.8 copy-start.98
  241.8 126.6 %copy-start.104 = (f32[2,256]{1,0:T(2,128)}, f32[2,256]{1,0:T(2,128)S(1)}, u32[]{:S(2)}) copy-start(f32[2,256]{1,0:T(2,128)S(1)} %broadcast_multiply_fusion.5) | copy-start | bytes 6148
  252.5 115.9 %copy-start.112 = (f32[2,256]{1,0:T(2,128)}, f32[2,256]{1,0:T(2,128)S(1)}, u32[]{:S(2)}) copy-start(f32[2,256]{1,0:T(2,128)S(1)} %add_rsqrt_fusion.1) | copy-start | bytes 6148
  252.5 12.5 copy-start.139
  253.9 30.8 %reduce-scatter.22.cloned.1.call-start = ((), (), s32[]{:S(2)}) async-start(), calls=%async_computation.22 | async-start | bytes 2359296 | tf_op jit(solution)/shard_map/reduce_scatter | solution.py:133
  274.3 10.4 copy-start.15
  274.3 10.4 copy-start.100
  274.3 25.5 %all-gather.19.cloned.1.call-start = ((), (), s32[]{:S(2)}) async-start(), calls=%async_computation.24 | async-start | bytes 2359296 | tf_op jit(solution)/shard_map/all_gather | solution.py:129
  288.7 35.2 %reduce-scatter.26.cloned.1.call-start = ((), (), s32[]{:S(2)}) async-start(), calls=%async_computation.25 | async-start | bytes 2359296 | tf_op jit(solution)/shard_map/reduce_scatter | solution.py:133
  313.6 29.3 %all-gather.21.cloned.1.call-start = ((), (), s32[]{:S(2)}) async-start(), calls=%async_computation.26 | async-start | bytes 2359296 | tf_op jit(solution)/shard_map/all_gather | solution.py:193
  331.7 36.7 %reduce-scatter.28.cloned.1.call-start = ((), (), s32[]{:S(2)}) async-start(), calls=%async_computation.27 | async-start | bytes 2359296 | tf_op jit(solution)/shard_map/reduce_scatter | solution.py:205
  358.0 29.6 %all-gather.23.cloned.1.call-start = ((), (), s32[]{:S(2)}) async-start(), calls=%async_computation.28 | async-start | bytes 2359296 | tf_op jit(solution)/shard_map/all_gather | solution.py:214
  358.0 14.5 %copy-start.115 = (f32[2,256]{1,0:T(2,128)}, f32[2,256]{1,0:T(2,128)S(1)}, u32[]{:S(2)}) copy-start(f32[2,256]{1,0:T(2,128)S(1)} %broadcast_multiply_fusion.4) | copy-start | bytes 6148
  376.4 63.3 %reduce-scatter.30.cloned.1.call-start = ((), (), s32[]{:S(2)}) async-start(), calls=%async_computation.29 | async-start | bytes 2359296 | tf_op jit(solution)/shard_map/reduce_scatter | solution.py:240
  429.3 10.4 copy-start.109
  429.4 28.7 %all-gather.27.cloned.1.call-start = ((), (), s32[]{:S(2)}) async-start(), calls=%async_computation.33 | async-start | bytes 2359296 | tf_op jit(solution)/shard_map/all_gather | solution.py:193
  443.0 24.8 %slice-start = ((s8[4718592]{0:T(1024)(128)(4,1)}), s8[524288]{0:T(1024)(128)(4,1)S(1)}, s32[]{:S(2)}) async-start(s8[4718592]{0:T(1024)(128)(4,1)} %bitcast.486), calls=%async_computation.41 | async-start | bytes 1048576
  445.2 12.9 copy-start.138
  446.8 35.2 %reduce-scatter.36.cloned.1.call-start = ((), (), s32[]{:S(2)}) async-start(), calls=%async_computation.34 | async-start | bytes 2359296 | tf_op jit(solution)/shard_map/reduce_scatter | solution.py:205
  458.0 9.8 slice-start.1
  467.9 14.2 %copy-start.87 = (f32[768]{0:T(1024)S(1)}, f32[768]{0:T(1024)}, u32[]{:S(2)}) copy-start(f32[768]{0:T(1024)} %copy-done.86) | copy-start | bytes 9220
  467.9 14.2 %copy-start.95 = (f32[768]{0:T(1024)S(1)}, f32[768]{0:T(1024)}, u32[]{:S(2)}) copy-start(f32[768]{0:T(1024)} %copy-done.94) | copy-start | bytes 9220
  467.9 14.2 %copy-start.111 = (f32[2,256]{1,0:T(2,128)S(1)}, f32[2,256]{1,0:T(2,128)}, u32[]{:S(2)}) copy-start(f32[2,256]{1,0:T(2,128)} %copy-done.110) | copy-start | bytes 6148
  471.7 10.4 copy-start.3
  471.7 10.4 copy-start.13
  471.7 10.4 copy-start.103
  471.7 13.2 %copy-start.118 = (f32[2,256]{1,0:T(2,128)S(1)}, f32[2,256]{1,0:T(2,128)}, u32[]{:S(2)}) copy-start(f32[2,256]{1,0:T(2,128)} %copy-done.117) | copy-start | bytes 6148
  471.7 27.7 %all-gather.29.cloned.1.call-start = ((), (), s32[]{:S(2)}) async-start(), calls=%async_computation.35 | async-start | bytes 2359296 | tf_op jit(solution)/shard_map/all_gather | solution.py:214
  487.1 12.3 copy-start.147
  488.2 238.0 %reduce-scatter.38.cloned.1.call-start = ((), (), s32[]{:S(2)}) async-start(), calls=%async_computation.36 | async-start | bytes 2359296 | tf_op jit(solution)/shard_map/reduce_scatter | solution.py:240
  543.0 253.9 %all-reduce.8.cloned.1.call-start = ((), (), s32[]{:S(2)}) async-start(), calls=%async_computation.40 | async-start | bytes 14155776
  565.6 363.3 %reduce-scatter.40.cloned.1.call-start = ((), (), s32[]{:S(2)}) async-start(), calls=%async_computation.37 | async-start | bytes 2506752 | tf_op jit(solution)/shard_map/reduce_scatter | solution.py:326
  571.9 534.2 %reduce-scatter.44.cloned.1.call-start = ((), (), s32[]{:S(2)}) async-start(), calls=%async_computation.39 | async-start | bytes 10027008 | tf_op jit(solution)/shard_map/reduce_scatter | solution.py:328
  573.8 4.7 copy-start.68
  585.7 5.5 copy-start.66
  585.7 696.3 %reduce-scatter.42.cloned.1.call-start = ((), (), s32[]{:S(2)}) async-start(), calls=%async_computation.38 | async-start | bytes 10027008 | tf_op jit(solution)/shard_map/reduce_scatter | solution.py:327
  585.9 5.2 copy-start.54
  604.4 121.7 %copy-start.26 = (f32[2,256,768]{2,1,0:T(8,128)S(1)}, f32[2,256,768]{2,1,0:T(8,128)}, u32[]{:S(2)}) copy-start(f32[2,256,768]{2,1,0:T(8,128)} %copy-done.25) | copy-start | bytes 4718596
  604.6 44.6 %copy-start.40 = (bf16[2,512,384]{1,2,0:T(8,128)(2,1)S(1)}, bf16[2,512,384]{1,2,0:T(8,128)(2,1)}, u32[]{:S(2)}) copy-start(bf16[2,512,384]{1,2,0:T(8,128)(2,1)} %get-tuple-element.274) | copy-start | bytes 2359300
  (143 other events, 279.5 us)
Sparse Core Ops, SparseCore 0:
  9.6 12.4 all-gather.10
  65.6 10.2 reduce-scatter.15
  83.1 10.2 reduce-scatter.31
  96.8 10.9 all-gather.12
  117.2 10.2 reduce-scatter.17
  132.4 10.9 all-gather.24
  157.2 10.2 reduce-scatter.33
  172.5 10.9 all-gather.14
  224.0 10.2 reduce-scatter.19
  240.2 10.2 reduce-scatter.23
  254.0 10.9 all-gather.16
  274.5 10.2 reduce-scatter.21
  288.8 10.9 all-gather.18
  313.7 10.2 reduce-scatter.25
  331.8 10.9 all-gather.20
  358.1 10.2 reduce-scatter.27
  376.6 10.9 all-gather.22
  429.5 10.2 reduce-scatter.29
  447.0 10.9 all-gather.26
  471.8 10.1 reduce-scatter.35
  488.3 11.0 all-gather.28
  543.1 10.2 reduce-scatter.37
  565.7 231.1 all-reduce.7
  802.2 126.6 reduce-scatter.39
  936.2 169.9 reduce-scatter.43
  1112.3 169.7 reduce-scatter.41
where the time goes:
time: 1300 us; the launch traced here: 1290 us
  waiting for transfers between devices  741 us (57%)
  matrix products  229 us (18%)
  blocking collectives  120 us (9%)
  local copies, waits for them, and re-layouts  90.5 us (7%)
  other arithmetic  86.7 us (7%)
  between operations  16.5 us (1%)
    reduce_scatter x1, waiting for transfers between devices, shards(): lax.psum_scatter(stacked[11], 'dp', scatter_dimension=1, tiled=True)  177 us
    reduce_scatter x1, waiting for transfers between devices, shards(): lax.psum_scatter(stacked[9], 'dp', scatter_dimension=1, tiled=True)  176 us
    reduce_scatter x1, waiting for transfers between devices, shards(): lax.psum_scatter(stacked[5], 'dp', scatter_dimension=1, tiled=True)  127 us
    psum x1, blocking collectives, shards(): columns = lax.psum((stacked[1], stacked[4], stacked[10]), 'dp')  76.7 us
    unnamed x27, waiting for transfers between devices  69.3 us
    all_gather x4, waiting for transfers between devices, forward_layer(): lax.all_gather(normed.astype(jnp.bfloat16), 'mp', axis=1, tiled=True)  43.8 us
    psum x1, blocking collectives, shards(): lax.psum((stacked[6], stacked[7], stacked[8], stacked[12], stacked[13], s...  43.8 us
    reduce_scatter x4, waiting for transfers between devices, forward_layer(): lax.psum_scatter(partial_down.astype(jnp.bfloat16), 'mp', scatter_dimensi...  38.6 us
  transfers between devices with their start and end apart: 26, of which 23 were waited for; matrix products, arithmetic and copies ran while one was open for 8% of the time, Pallas kernels for 0%

commit v1 on v0

v1 whole, which is shorter than its diff:
```python
import functools

import jax
import jax.numpy as jnp
from jax import lax
from jax.experimental import pallas as pl
from jax.experimental.pallas import tpu as pltpu
from jax.sharding import PartitionSpec as P

DH = 64
QSLOT = 32
BF = jnp.bfloat16
F32 = jnp.float32
PAIR = 2 * DH
CHUNK = 256


def nn(left, right):
    return lax.dot_general(left, right, (((1,), (0,)), ((), ())), preferred_element_type=F32)


def nt(left, right):
    return lax.dot_general(left, right, (((1,), (1,)), ((), ())), preferred_element_type=F32)


def tn(left, right):
    return lax.dot_general(left, right, (((0,), (0,)), ((), ())), preferred_element_type=F32)


def beside(*refs):
    return jnp.concatenate([r[...] for r in refs], axis=1)


def whole(*shape):
    return pl.BlockSpec(shape, lambda i: (0,) * len(shape))


def columns(rows, width):
    return pl.BlockSpec((rows, width), lambda i: (0, i))


def layer_columns(layer, rows, width):
    return pl.BlockSpec((None, rows, width), lambda i: (layer, 0, i))


def layer_whole(layer, rows, width):
    return pl.BlockSpec((None, rows, width), lambda i: (layer, 0, 0))


def sds(shape, dtype):
    return jax.ShapeDtypeStruct(shape, dtype)


def params(megabytes):
    return pltpu.CompilerParams(vmem_limit_bytes=megabytes * 1024 * 1024)


def attend_kernel(
    segq, segk, x, wqo, wqp, wko, wkp, wvo, wvp, bqo, bqp, bvo, bvp,
    qo, qp, ko, kp, vo, vp, co, cp, lse, bias,
):
    @pl.when(pl.program_id(0) == 0)
    def _():
        bias[...] = jnp.where(segq[...] == segk[...], 0.0, -1e9)

    xv = x[...]
    q = (nn(xv, beside(wqo, wqp)) + beside(bqo, bqp)).astype(BF)
    k = nn(xv, beside(wko, wkp)).astype(BF)
    v = (nn(xv, beside(wvo, wvp)) + beside(bvo, bvp)).astype(BF)
    first = lax.broadcasted_iota(jnp.int32, (1, PAIR), 1) < DH
    lse[...] = jnp.zeros_like(lse)
    for pair, (qr, kr, vr, cr) in enumerate(((qo, ko, vo, co), (qp, kp, vp, cp))):
        at = slice(pair * PAIR, (pair + 1) * PAIR)
        qq, kk, vv = q[:, at], k[:, at], v[:, at]
        qr[...] = qq
        kr[...] = kk
        vr[...] = vv
        outs, peaks = [], []
        for head in range(2):
            mine = first if head == 0 else ~first
            qm = jnp.where(mine, qq, jnp.zeros_like(qq)) * 0.125
            s = nt(qm.astype(BF), kk) + bias[...]
            peak = jnp.max(s, axis=1, keepdims=True)
            e = jnp.exp(s - peak).astype(BF)
            outs.append(nn(e, jnp.where(mine, vv, jnp.ones_like(vv))))
            peaks.append(peak)
        total = pltpu.roll(jnp.where(first, outs[1], outs[0]), DH, 1)
        cr[...] = (jnp.where(first, outs[0], outs[1]) / total).astype(BF)
        logs = jnp.where(first, peaks[0], peaks[1]) + jnp.log(total)
        flat = logs.T
        lse[2 * pair : 2 * pair + 1, :] = flat[0:1, :]
        lse[2 * pair + 1 : 2 * pair + 2, :] = flat[DH : DH + 1, :]


def attend(layer, segq, segk, x, own, peer, biases):
    slots, width = x.shape
    half = own["w_query"].shape[2]
    steps = half // PAIR
    weight = layer_columns(layer, width, PAIR)
    act = columns(slots, PAIR)
    bias = columns(1, PAIR)
    ins = [whole(slots, 1), whole(1, slots), whole(slots, width)] + [weight] * 6 + [bias] * 4
    return pl.pallas_call(
        attend_kernel,
        grid=(steps,),
        in_specs=ins,
        out_specs=[act] * 8 + [pl.BlockSpec((None, 8, slots), lambda i: (i, 0, 0))],
        out_shape=[sds((slots, half), BF)] * 8 + [sds((steps, 8, slots), F32)],
        scratch_shapes=[pltpu.VMEM((slots, slots), F32)],
        compiler_params=params(48),
    )(
        segq, segk, x,
        own["w_query"], peer["w_query"], own["w_key"], peer["w_key"], own["w_value"], peer["w_value"],
        *biases,
    )


def normalize(r):
    mean = jnp.mean(r, axis=1, keepdims=True)
    c = r - mean
    rstd = lax.rsqrt(jnp.mean(c * c, axis=1, keepdims=True) + 1e-12)
    return c * rstd, rstd


def feed_kernel(
    x, co, cp, woo, wop, b_out, g1, s1, wuo, wup, wdo, wdp, buo, bup, b_down, g2, s2,
    n1, rstd1, hlow, acto, actp, gpo, gpp, n2, rstd2, y, h, acc,
):
    step = pl.program_id(0)

    @pl.when(step == 0)
    def _():
        att = nt(co[...], woo[...]) + nt(cp[...], wop[...]) + b_out[...]
        n, rstd = normalize(x[...].astype(F32) + att)
        n1[...] = n
        rstd1[...] = rstd
        hv = n * g1[...] + s1[...]
        h[...] = hv
        hlow[...] = hv.astype(BF)
        acc[...] = jnp.zeros_like(acc)

    u = nn(hlow[...], beside(wuo, wup)) + beside(buo, bup)
    cdf = 0.5 * (1.0 + lax.erf(u * 0.7071067811865476))
    act = (u * cdf).astype(BF)
    slope = (cdf + u * (jnp.exp(u * u * -0.5) * 0.3989422804014327)).astype(BF)
    acto[...] = act[:, :CHUNK]
    actp[...] = act[:, CHUNK:]
    gpo[...] = slope[:, :CHUNK]
    gpp[...] = slope[:, CHUNK:]
    acc[...] += nt(act, beside(wdo, wdp))

    @pl.when(step == pl.num_programs(0) - 1)
    def _():
        n, rstd = normalize(h[...] + (acc[...] + b_down[...]))
        n2[...] = n
        rstd2[...] = rstd
        y[...] = (n * g2[...] + s2[...]).astype(BF)


def feed(layer, x, ctx_own, ctx_peer, own, peer, vec, up_biases):
    slots, width = x.shape
    half = own["w_query"].shape[2]
    ff = own["w_up"].shape[2]
    weight = layer_columns(layer, width, CHUNK)
    full = whole(slots, width)
    row = whole(1, width)
    one = whole(slots, 1)
    ins = [full, whole(slots, half), whole(slots, half)]
    ins += [layer_whole(layer, width, half)] * 2 + [row] * 3 + [weight] * 4
    ins += [columns(1, CHUNK)] * 2 + [row] * 3
    outs = [full, one, full] + [columns(slots, CHUNK)] * 4 + [full, one, full]
    shapes = [sds((slots, width), F32), sds((slots, 1), F32), sds((slots, width), BF)]
    shapes += [sds((slots, ff), BF)] * 4
    shapes += [sds((slots, width), F32), sds((slots, 1), F32), sds((slots, width), BF)]
    return pl.pallas_call(
        feed_kernel,
        grid=(ff // CHUNK,),
        in_specs=ins,
        out_specs=outs,
        out_shape=shapes,
        scratch_shapes=[pltpu.VMEM((slots, width), F32)] * 2,
        compiler_params=params(56),
    )(
        x, ctx_own, ctx_peer, own["w_out"], peer["w_out"], vec["b_out"], vec["first_gain"], vec["first_shift"],
        own["w_up"], peer["w_up"], own["w_down"], peer["w_down"], *up_biases,
        vec["b_down"], vec["second_gain"], vec["second_shift"],
    )


def norm_back(dy, n, rstd, gain):
    gdy = dy * gain
    return (
        gdy - jnp.mean(gdy, axis=1, keepdims=True) - n * jnp.mean(gdy * n, axis=1, keepdims=True)
    ) * rstd


def colsum(v):
    return jnp.sum(v.astype(F32), axis=0, keepdims=True)


def norm_kernel(dy, n, rstd, gain, dr, low, sums):
    dv = dy[...].astype(F32)
    nv = n[...]
    r = norm_back(dv, nv, rstd[...], gain[...])
    lowv = r.astype(BF)
    dr[...] = r
    low[...] = lowv
    sums[...] = jnp.concatenate(
        [colsum(dv * nv), colsum(dv), colsum(lowv), jnp.zeros((5, dv.shape[1]), F32)], axis=0
    )


def norm_backward(dy, n, rstd, gain):
    slots, width = n.shape
    return pl.pallas_call(
        norm_kernel,
        out_shape=[sds((slots, width), F32), sds((slots, width), BF), sds((8, width), F32)],
        compiler_params=params(32),
    )(dy, n, rstd, gain)


def feed_back_kernel(
    dff, dr2, wdo, wdp, wuo, wup, gpo, gpp, n1, rstd1, g1,
    duo, dup, gbuo, gbup, dr1, datt, sums, acc,
):
    step = pl.program_id(0)
    dact = nn(dff[...], beside(wdo, wdp))
    du = (dact * beside(gpo, gpp).astype(F32)).astype(BF)
    duo[...] = du[:, :CHUNK]
    dup[...] = du[:, CHUNK:]
    total = colsum(du)
    gbuo[...] = total[:, :CHUNK]
    gbup[...] = total[:, CHUNK:]
    part = nt(du, beside(wuo, wup))

    @pl.when(step == 0)
    def _():
        acc[...] = dr2[...] + part

    @pl.when(step > 0)
    def _():
        acc[...] += part

    @pl.when(step == pl.num_programs(0) - 1)
    def _():
        dh = acc[...]
        n = n1[...]
        r = norm_back(dh, n, rstd1[...], g1[...])
        low = r.astype(BF)
        dr1[...] = r
        datt[...] = low
        sums[...] = jnp.concatenate(
            [colsum(dh * n), colsum(dh), colsum(low), jnp.zeros((5, dh.shape[1]), F32)], axis=0
        )


def feed_back(layer, dff, dr2, own, peer, slope_own, slope_peer, n1, rstd1, gain):
    slots, width = dff.shape
    ff = own["w_up"].shape[2]
    weight = layer_columns(layer, width, CHUNK)
    act = columns(slots, CHUNK)
    full = whole(slots, width)
    ins = [full, full] + [weight] * 4 + [act] * 2 + [full, whole(slots, 1), whole(1, width)]
    return pl.pallas_call(
        feed_back_kernel,
        grid=(ff // CHUNK,),
        in_specs=ins,
        out_specs=[act] * 2 + [columns(1, CHUNK)] * 2 + [full, full, whole(8, width)],
        out_shape=[sds((slots, ff), BF)] * 2
        + [sds((1, ff), F32)] * 2
        + [sds((slots, width), F32), sds((slots, width), BF), sds((8, width), F32)],
        scratch_shapes=[pltpu.VMEM((slots, width), F32)],
        compiler_params=params(56),
    )(
        dff, dr2, own["w_down"], peer["w_down"], own["w_up"], peer["w_up"],
        slope_own, slope_peer, n1, rstd1, gain,
    )


def attend_back_kernel(
    segk, segq, datt, dr1, woo, wop, wqo, wqp, wko, wkp, wvo, wvp,
    qo, qp, ko, kp, vo, vp, lse,
    dqo, dqp, dko, dkp, dvo, dvp, gbqo, gbqp, gbvo, gbvp, dx, bias,
):
    step = pl.program_id(0)

    @pl.when(step == 0)
    def _():
        bias[...] = jnp.where(segk[...] == segq[...], 0.0, -1e9)

    dctx = nn(datt[...], beside(woo, wop)).astype(BF)
    first = lax.broadcasted_iota(jnp.int32, (1, PAIR), 1) < DH
    grads = []
    for pair, (qr, kr, vr, dqr, dkr, dvr, gbq, gbv) in enumerate(
        ((qo, ko, vo, dqo, dko, dvo, gbqo, gbvo), (qp, kp, vp, dqp, dkp, dvp, gbqp, gbvp))
    ):
        qq, kk, vv = qr[...], kr[...], vr[...]
        do = dctx[:, pair * PAIR : (pair + 1) * PAIR]
        dq_t, dk, dv = 0.0, 0.0, 0.0
        for head in range(2):
            mine = first if head == 0 else ~first
            qm = (jnp.where(mine, qq, jnp.zeros_like(qq)) * 0.125).astype(BF)
            km = (jnp.where(mine, kk, jnp.zeros_like(kk)) * 0.125).astype(BF)
            dom = jnp.where(mine, do, jnp.zeros_like(do))
            at = 2 * pair + head
            p = jnp.exp(nt(kk, qm) + bias[...] - lse[at : at + 1, :])
            dp = nt(vv, dom)
            delta = jnp.sum(p * dp, axis=0, keepdims=True)
            ds = (p * (dp - delta)).astype(BF)
            dv += nn(p.astype(BF), dom)
            dk += nn(ds, qm)
            dq_t += nn(km.T, ds)
        dq = dq_t.T.astype(BF)
        dk = dk.astype(BF)
        dv = dv.astype(BF)
        dqr[...] = dq
        dkr[...] = dk
        dvr[...] = dv
        gbq[...] = colsum(dq)
        gbv[...] = colsum(dv)
        grads.append((dq, dk, dv))
    back = jnp.concatenate([g[i] for i in range(3) for g in grads], axis=1)
    part = nt(back, beside(wqo, wqp, wko, wkp, wvo, wvp))

    @pl.when(step == 0)
    def _():
        dx[...] = dr1[...] + part

    @pl.when(step > 0)
    def _():
        dx[...] += part


def attend_back(layer, segk, segq, datt, dr1, own, peer, saved, lse):
    slots, width = datt.shape
    half = own["w_query"].shape[2]
    steps = half // PAIR
    weight = layer_columns(layer, width, PAIR)
    act = columns(slots, PAIR)
    full = whole(slots, width)
    ins = [whole(slots, 1), whole(1, slots), full, full] + [weight] * 8 + [act] * 6
    ins += [pl.BlockSpec((None, 8, slots), lambda i: (i, 0, 0))]
    return pl.pallas_call(
        attend_back_kernel,
        grid=(steps,),
        in_specs=ins,
        out_specs=[act] * 6 + [columns(1, PAIR)] * 4 + [full],
        out_shape=[sds((slots, half), BF)] * 6 + [sds((1, half), F32)] * 4 + [sds((slots, width), F32)],
        scratch_shapes=[pltpu.VMEM((slots, slots), F32)],
        compiler_params=params(56),
    )(
        segk, segq, datt, dr1, own["w_out"], peer["w_out"],
        own["w_query"], peer["w_query"], own["w_key"], peer["w_key"], own["w_value"], peer["w_value"],
        *saved, lse,
    )


def swap(value):
    return lax.ppermute(value, "mp", [(0, 1), (1, 0)])


def flip(value, bit, size):
    return lax.ppermute(value, "dp", [(i, i ^ (1 << bit)) for i in range(size)])


def scatter_sum(grad, order, size):
    bits = size.bit_length() - 1
    me = lax.axis_index("dp")
    value = grad.astype(BF).reshape((2,) * bits + (grad.shape[0] // size, grad.shape[1]))
    left = list(range(bits - 1, -1, -1))
    for bit in order:
        axis = left.index(bit)
        left.pop(axis)
        mine = (me >> bit) & 1
        keep = lax.dynamic_index_in_dim(value, mine, axis, keepdims=False)
        send = lax.dynamic_index_in_dim(value, 1 - mine, axis, keepdims=False)
        got = flip(send, bit, size)
        value = keep.astype(F32) + got.astype(F32)
        if left:
            value = value.astype(BF)
    return value


def full_sum(value, size):
    for bit in range(size.bit_length() - 1):
        value = value + flip(value, bit, size)
    return value


NAMES = (
    "w_query", "b_query", "w_key", "w_value", "b_value", "w_out", "b_out", "first_gain", "first_shift",
    "w_up", "b_up", "w_down", "b_down", "second_gain", "second_shift",
)


def shards(dp, tokens, lengths, cotangent, *given):
    held = dict(zip(NAMES, given, strict=True))
    layers, width, half = held["w_query"].shape
    ff = held["w_up"].shape[2]
    slots = 2 * tokens.shape[1]
    me = lax.axis_index("mp")

    def pick(array, index):
        return lax.dynamic_index_in_dim(array, index, 0, keepdims=False)

    def take_row(array):
        return jnp.concatenate([pick(array, me), swap(pick(array, 1 - me))], axis=0)

    def give_row(value):
        cut = slots // 2
        mine, other = value[:cut], swap(value[cut:])
        return jnp.stack([jnp.where(me == 0, mine, other), jnp.where(me == 0, other, mine)])

    x = take_row(tokens)
    matrices = ("w_query", "w_key", "w_value", "w_out", "w_up", "w_down")
    peer = {name: swap(held[name]) for name in matrices[:3]}
    halves = jnp.concatenate([held["b_query"], held["b_value"], held["b_up"]], axis=1)
    halves_peer = swap(halves)
    for name in matrices[3:]:
        peer[name] = swap(held[name])
    dy = take_row(cotangent)

    row_lengths = pick(lengths, me)
    slot = lax.rem(jnp.arange(slots, dtype=jnp.int32) + me * (slots // 2), slots)
    seg_width = jnp.where(row_lengths[1] > 0, QSLOT, slots)
    segment = lax.div(slot, seg_width)
    inside = slot - segment * seg_width
    onehot = segment[:, None] == jnp.arange(lengths.shape[1], dtype=jnp.int32)[None, :]
    live = inside < jnp.sum(jnp.where(onehot, row_lengths[None, :], 0), axis=1)
    segk = jnp.where(live, segment, -1)
    segq_c, segq_r = segment[:, None], segment[None, :]
    segk_c, segk_r = segk[:, None], segk[None, :]

    def vectors(layer):
        names = ("b_out", "first_gain", "first_shift", "b_down", "second_gain", "second_shift")
        return {n: held[n][layer].astype(F32)[None, :] for n in names}

    kept = []
    for layer in range(layers):
        mine = halves[layer].astype(F32)[None, :]
        theirs = halves_peer[layer].astype(F32)[None, :]
        qv = (mine[:, :half], theirs[:, :half], mine[:, half : 2 * half], theirs[:, half : 2 * half])
        up = (mine[:, 2 * half :], theirs[:, 2 * half :])
        vec = vectors(layer)
        att = attend(layer, segq_c, segk_r, x, held, peer, qv)
        fed = feed(layer, x, att[6], att[7], held, peer, vec, up)
        kept.append((x, att, fed, vec))
        x = fed[-1]

    encoded = give_row(x)
    grad_shards = {name: [None] * layers for name in matrices}
    small = [None] * layers

    def weight_grad(left, right_own, right_peer, left_peer=None):
        left_peer = swap(left) if left_peer is None else left_peer
        return tn(left, right_own) + tn(left_peer, swap(right_peer))

    bits = dp.bit_length() - 1
    rest = tuple(range(4, bits)) if bits > 4 else ()

    def order(*head):
        return tuple(b for b in head if b < bits) + rest

    for layer in reversed(range(layers)):
        x_in, att, fed, vec = kept[layer]
        (qo, qp, ko, kp, vo, vp, ctx_own, ctx_peer, lse) = att
        (n1, rstd1, hlow, act_own, act_peer, slope_own, slope_peer, n2, rstd2, _) = fed
        dr2, dff, sums2 = norm_backward(dy, n2, rstd2, vec["second_gain"])
        grad_down = weight_grad(dff, act_own, act_peer)
        grad_shards["w_down"][layer] = scatter_sum(grad_down, order(0, 1, 2, 3), dp)
        du_own, du_peer, gbu_own, gbu_peer, dr1, datt, sums1 = feed_back(
            layer, dff, dr2, held, peer, slope_own, slope_peer, n1, rstd1, vec["first_gain"]
        )
        grad_up = weight_grad(hlow, du_own, du_peer)
        grad_shards["w_up"][layer] = scatter_sum(grad_up, order(1, 0, 2, 3), dp)
        grad_out = weight_grad(datt, ctx_own, ctx_peer)
        grad_shards["w_out"][layer] = scatter_sum(grad_out, order(0, 1, 2, 3), dp)
        back = attend_back(
            layer, segk_c, segq_r, datt, dr1, held, peer, (qo, qp, ko, kp, vo, vp), lse
        )
        dqo, dqp, dko, dkp, dvo, dvp, gbq_own, gbq_peer, gbv_own, gbv_peer, dy = back
        x_peer = swap(x_in)
        for name, own_part, peer_part, way in (
            ("w_query", dqo, dqp, (2, 3, 0, 1)),
            ("w_key", dko, dkp, (2, 3, 1, 0)),
            ("w_value", dvo, dvp, (1, 0, 2, 3)),
        ):
            grad = weight_grad(x_in, own_part, peer_part, x_peer)
            grad_shards[name][layer] = scatter_sum(grad, order(*way), dp)
        rows = jnp.concatenate([sums1[:3].reshape(1, -1), sums2[:3].reshape(1, -1)], axis=1)
        mine = jnp.concatenate([gbq_own, gbv_own, gbu_own, rows], axis=1)
        theirs = jnp.concatenate([gbq_peer, gbv_peer, gbu_peer, rows], axis=1)
        small[layer] = full_sum(mine + swap(theirs), dp)

    token_grad = give_row(dy.astype(BF)).astype(F32)
    stacked = {name: jnp.stack(grad_shards[name]) for name in matrices}
    packed = jnp.concatenate(small, axis=0)
    cuts = [half, half, ff] + [width] * 6
    pieces, at = [], 0
    for cut in cuts:
        pieces.append(packed[:, at : at + cut])
        at += cut
    gbq, gbv, gbu, gfg, gfs, gbo, gsg, gss, gbd = pieces
    return (
        encoded, token_grad, stacked["w_query"], gbq, stacked["w_key"], stacked["w_value"], gbv,
        stacked["w_out"], gbo, gfg, gfs, stacked["w_up"], gbu, stacked["w_down"], gbd, gsg, gss,
    )


def solution(mesh):
    cols, mats, rep = P(None, "mp"), P(None, None, "mp"), P()
    placed = (
        P("dp", "mp", None), P("dp", None), P("dp", "mp", None),
        mats, cols, mats, mats, cols, mats, rep, rep, rep, mats, cols, mats, rep, rep, rep,
    )
    grads = P(None, "dp", "mp")
    return jax.shard_map(
        functools.partial(shards, mesh.shape["dp"]),
        mesh=mesh,
        in_specs=placed,
        out_specs=(
            P("dp", "mp", None), P("dp", "mp", None), grads, cols, grads, grads, cols,
            grads, rep, rep, rep, grads, cols, grads, rep, rep, rep,
        ),
        check_vma=False,
    )
```

time: 1300 us -> 511 us (0.39)
  waiting for transfers between devices: 741 us -> 223 us
  matrix products: 229 us -> 21.5 us
  blocking collectives: 120 us -> 0 us
  Pallas kernels: 0 us -> 119 us
  starting transfers between devices: 3.44 us -> 72.3 us
  other arithmetic: 86.7 us -> 23.2 us
  local copies, waits for them, and re-layouts: 90.5 us -> 44.1 us
  between operations: 16.5 us -> 3.41 us
    reduce_scatter x15 -> x0, waiting for transfers between devices: 564 us -> none  [the longest x1 177 us: shards(): lax.psum_scatter(stacked[11], 'dp', scatter_dimension=1, tiled=True)]
    ppermute x0 -> x89, waiting for transfers between devices: none -> 223 us  [the longest x56 217 us: flip(): return lax.ppermute(value, 'dp', [(i, i ^ 1 << bit) for i in range(size)])]
    dot_general x72 -> x24, matrix products: 204 us -> 21.5 us  [tn(): lax.dot_general(left, right, (((0,), (0,)), ((), ())), preferred_element_...]
    psum x2 -> x0, blocking collectives: 120 us -> none  [the longest x1 76.7 us: shards(): columns = lax.psum((stacked[1], stacked[4], stacked[10]), 'dp')]
    pallas_call x0 -> x10, Pallas kernels: none -> 119 us  [the longest x2 35.7 us: attend_back(): pl.pallas_call(attend_back_kernel, grid=(steps,), in_specs=ins, out_specs...]
    all_gather x10 -> x0, waiting for transfers between devices: 107 us -> none  [the longest x4 43.8 us: forward_layer(): lax.all_gather(normed.astype(jnp.bfloat16), 'mp', axis=1, tiled=True)]
    ppermute x0 -> x89, starting transfers between devices: none -> 72.3 us  [the longest x56 63.9 us: flip(): return lax.ppermute(value, 'dp', [(i, i ^ 1 << bit) for i in range(size)])]
    unnamed x27 -> x0, waiting for transfers between devices: 69.3 us -> none
  transfers between devices with their start and end apart: 26 -> 89, of which waited for: 23 -> 49; matrix products, arithmetic and copies ran while one was open for 8% -> 12% of each run, Pallas kernels for 0% -> 24%
where the time goes in v1:
time: 511 us; the launch traced here: 506 us
  waiting for transfers between devices  223 us (44%)
  Pallas kernels  119 us (23%)
  starting transfers between devices  72.3 us (14%)
  local copies, waits for them, and re-layouts  44.1 us (9%)
  other arithmetic  23.2 us (5%)
  matrix products  21.5 us (4%)
    ppermute x56, waiting for transfers between devices, flip(): return lax.ppermute(value, 'dp', [(i, i ^ 1 << bit) for i in range(size)])  217 us
    ppermute x56, starting transfers between devices, flip(): return lax.ppermute(value, 'dp', [(i, i ^ 1 << bit) for i in range(size)])  63.9 us
    pallas_call x2, Pallas kernels, attend_back(): pl.pallas_call(attend_back_kernel, grid=(steps,), in_specs=ins, out_specs...  35.7 us
    pallas_call x2, Pallas kernels, feed(): pl.pallas_call(feed_kernel, grid=(ff // CHUNK,), in_specs=ins, out_specs=...  33 us
    unnamed x196, local copies, waits for them, and re-layouts  32.8 us
    pallas_call x2, Pallas kernels, feed_back(): pl.pallas_call(feed_back_kernel, grid=(ff // CHUNK,), in_specs=ins, out_s...  28.9 us
    dot_general x24, matrix products, tn(): lax.dot_general(left, right, (((0,), (0,)), ((), ())), preferred_element_...  21.5 us
    pallas_call x2, Pallas kernels, attend(): pl.pallas_call(attend_kernel, grid=(steps,), in_specs=ins, out_specs=[act...  19.5 us
  transfers between devices with their start and end apart: 89, of which 49 were waited for; matrix products, arithmetic and copies ran while one was open for 12% of the time, Pallas kernels for 24%

profile of v1, /device:TPU:0, one launch (start us, length us, event | category | flops | bytes accessed | tf_op | source)
XLA Modules:
  0.0 506.2 jit_solution(13291421681352068933)
XLA Ops:
  1.3 2.0 dynamic-slice_bitcast_fusion.7
  5.8 2.0 dynamic-slice_bitcast_fusion.5
  11.1 1.6 collective-permute-done.4
  13.9 3.3 fusion.41
  23.0 9.8 %shard_map.305 = (bf16[512,384]{1,0:T(8,128)(2,1)S(1)}, bf16[512,384]{1,0:T(8,128)(2,1)S(1)}, bf16[512,384]{1,0:T(8,128)(2,1)S(1)}, bf16[512,384]{1,0:T(8,128)(2...) custom-call(s32[512,1]{1,0:T(8,128)S(1)} %get-tuple-element.248.segq, ...), custom_call_target="tpu_custom_call" | custom-call | tf_op jit(solution)/shard_map/pallas_call | solution.py:103
  40.5 16.3 %shard_map.306 = (f32[512,768]{1,0:T(8,128)}, f32[512,1]{1,0:T(8,128)}, bf16[512,768]{1,0:T(8,128)(2,1)}, bf16[512,1536]{1,0:T(8,128)(2,1)}, bf16[512,1536]{1,0:...) custom-call(bf16[512,768]{1,0:T(8,128)(2,1)} %copy-done.5, ...), custom_call_target="tpu_custom_call" | custom-call | tf_op jit(solution)/shard_map/pallas_call | solution.py:175
  58.0 9.7 %shard_map.307 = (bf16[512,384]{1,0:T(8,128)(2,1)S(1)}, bf16[512,384]{1,0:T(8,128)(2,1)S(1)}, bf16[512,384]{1,0:T(8,128)(2,1)S(1)}, bf16[512,384]{1,0:T(8,128)(2...) custom-call(s32[512,1]{1,0:T(8,128)S(1)} %get-tuple-element.248.segq, ...), custom_call_target="tpu_custom_call" | custom-call | tf_op jit(solution)/shard_map/pallas_call | solution.py:103
  74.3 16.7 %shard_map.308 = (f32[512,768]{1,0:T(8,128)}, f32[512,1]{1,0:T(8,128)}, bf16[512,768]{1,0:T(8,128)(2,1)}, bf16[512,1536]{1,0:T(8,128)(2,1)}, bf16[512,1536]{1,0:...) custom-call(bf16[512,768]{1,0:T(8,128)(2,1)} %get-tuple-element.99.x, ...), custom_call_target="tpu_custom_call" | custom-call | tf_op jit(solution)/shard_map/pallas_call | solution.py:175
  96.5 14.4 %shard_map.310 = (bf16[512,1536]{1,0:T(8,128)(2,1)}, bf16[512,1536]{1,0:T(8,128)(2,1)}, f32[1,1536]{1,0:T(1,128)}, f32[1,1536]{1,0:T(1,128)}, f32[512,768]{1,0:T...) custom-call(bf16[512,768]{1,0:T(8,128)(2,1)} %copy-done.6, f32[512,768]{1,0:T(8,128)} %copy-done.18, ...), custom_call_target="tpu_custom_call" | custom-call | tf_op jit(solution)/shard_map/pallas_call | solution.py:264
  111.0 17.8 %shard_map.311 = (bf16[512,384]{1,0:T(8,128)(2,1)}, bf16[512,384]{1,0:T(8,128)(2,1)}, bf16[512,384]{1,0:T(8,128)(2,1)}, bf16[512,384]{1,0:T(8,128)(2,1)}, bf16[5...) custom-call(s32[512,1]{1,0:T(8,128)} %get-tuple-element.247.segk, ...), custom_call_target="tpu_custom_call" | custom-call | tf_op jit(solution)/shard_map/pallas_call | solution.py:343
  136.5 14.5 %shard_map.313 = (bf16[512,1536]{1,0:T(8,128)(2,1)}, bf16[512,1536]{1,0:T(8,128)(2,1)}, f32[1,1536]{1,0:T(1,128)}, f32[1,1536]{1,0:T(1,128)}, f32[512,768]{1,0:T...) custom-call(bf16[512,768]{1,0:T(8,128)(2,1)} %copy-done.8, f32[512,768]{1,0:T(8,128)} %copy-done.17, ...), custom_call_target="tpu_custom_call" | custom-call | tf_op jit(solution)/shard_map/pallas_call | solution.py:264
  151.1 17.9 %shard_map.314 = (bf16[512,384]{1,0:T(8,128)(2,1)}, bf16[512,384]{1,0:T(8,128)(2,1)}, bf16[512,384]{1,0:T(8,128)(2,1)}, bf16[512,384]{1,0:T(8,128)(2,1)}, bf16[5...) custom-call(s32[512,1]{1,0:T(8,128)} %get-tuple-element.247.segk, ...), custom_call_target="tpu_custom_call" | custom-call | tf_op jit(solution)/shard_map/pallas_call | solution.py:343
  172.1 2.9 collective-permute-start.29
  176.8 2.1 collective-permute-start.30
  181.0 1.9 collective-permute-start.31
  185.6 2.9 collective-permute-start.32
  201.8 1.8 collective-permute-start.13
  208.2 3.5 collective-permute-done.13
  211.8 5.5 %collective-permute-done.34 = bf16[2,2,2,48,384]{4,3,2,1,0:T(8,128)(2,1)S(1)} collective-permute-done((bf16[2,2,2,48,384]{4,3,2,1,0:T(8,128)(2,1)S(1)}, bf16[2,2,2,48,384]{4,3,2,1,0:T(8,128)(2,1)S(1)}, u32[]{:S(2)}, u32[]{:S(2)}) %collective-permute-start.34) | collective-permute-done | bytes 294944 | tf_op jit(solution)/shard_map/ppermute | solution.py:363
  219.0 6.7 %collective-permute-done.44 = bf16[2,2,2,48,384]{4,3,0,1,2:T(8,128)(2,1)S(1)} collective-permute-done((bf16[2,2,2,48,384]{4,3,0,1,2:T(8,128)(2,1)S(1)}, bf16[2,2,2,48,384]{4,3,0,1,2:T(8,128)(2,1)S(1)}, u32[]{:S(2)}, u32[]{:S(2)}) %collective-permute-start.44) | collective-permute-done | bytes 294944 | tf_op jit(solution)/shard_map/ppermute | solution.py:363
  229.2 1.6 collective-permute-done.48
  234.1 1.9 collective-permute-start.14
  240.2 7.8 %collective-permute-done.14 = bf16[2,2,48,384]{3,2,0,1:T(8,128)(2,1)S(1)} collective-permute-done((bf16[2,2,48,384]{3,2,0,1:T(8,128)(2,1)S(1)}, bf16[2,2,48,384]{3,2,0,1:T(8,128)(2,1)S(1)}, u32[]{:S(2)}, u32[]{:S(2)}) %collective-permute-start.14) | collective-permute-done | bytes 147488 | tf_op jit(solution)/shard_map/ppermute | solution.py:363
  250.4 2.7 collective-permute-done.45
  254.7 2.7 collective-permute-done.15
  259.0 2.8 collective-permute-done.36
  261.9 4.3 collective-permute-done.46
  267.7 2.4 collective-permute-done.16
  271.7 2.4 collective-permute-done.37
  275.3 4.0 collective-permute-done.47
  281.4 4.6 collective-permute-done.19
  288.3 4.4 collective-permute-done.61
  292.8 3.1 collective-permute-done.55
  296.9 8.8 %collective-permute-done.20 = bf16[2,2,48,384]{3,2,0,1:T(8,128)(2,1)S(1)} collective-permute-done((bf16[2,2,48,384]{3,2,0,1:T(8,128)(2,1)S(1)}, bf16[2,2,48,384]{3,2,0,1:T(8,128)(2,1)S(1)}, u32[]{:S(2)}, u32[]{:S(2)}) %collective-permute-start.20) | collective-permute-done | bytes 147488 | tf_op jit(solution)/shard_map/ppermute | solution.py:363
  305.7 6.5 %collective-permute-done.40 = bf16[2,2,48,384]{3,2,1,0:T(8,128)(2,1)S(1)} collective-permute-done((bf16[2,2,48,384]{3,2,1,0:T(8,128)(2,1)S(1)}, bf16[2,2,48,384]{3,2,1,0:T(8,128)(2,1)S(1)}, u32[]{:S(2)}, u32[]{:S(2)}) %collective-permute-start.40) | collective-permute-done | bytes 147488 | tf_op jit(solution)/shard_map/ppermute | solution.py:363
  313.8 3.5 collective-permute-done.50
  319.0 3.5 collective-permute-done.62
  324.1 3.5 collective-permute-done.56
  329.3 2.7 collective-permute-done.21
  333.6 2.8 collective-permute-done.41
  336.4 4.3 collective-permute-done.51
  340.8 4.7 collective-permute-done.63
  345.5 4.3 collective-permute-done.57
  351.4 2.4 collective-permute-done.22
  355.4 2.4 collective-permute-done.42
  358.9 3.7 collective-permute-done.52
  363.8 3.7 collective-permute-done.64
  368.6 3.7 collective-permute-done.58
  385.4 1.8 add_convert_fusion
  387.5 1.6 collective-permute-start.85
  392.8 14.6 %collective-permute-done.73 = bf16[2,2,2,48,1536]{4,3,0,1,2:T(8,128)(2,1)S(1)} collective-permute-done((bf16[2,2,2,48,1536]{4,3,0,1,2:T(8,128)(2,1)S(1)}, bf16[2,2,2,48,1536]{4,3,0,1,2:T(8,128)(2,1)S(1)}, u32[]{:S(2)}, u32[]{:S(2)}) %collective-permute-start.73) | collective-permute-done | bytes 1179680 | tf_op jit(solution)/shard_map/ppermute | solution.py:363
  407.8 1.6 collective-permute-start.74
  409.5 22.4 %collective-permute-done.67 = bf16[2,2,2,48,1536]{4,3,0,1,2:T(8,128)(2,1)S(1)} collective-permute-done((bf16[2,2,2,48,1536]{4,3,0,1,2:T(8,128)(2,1)S(1)}, bf16[2,2,2,48,1536]{4,3,0,1,2:T(8,128)(2,1)S(1)}, u32[]{:S(2)}, u32[]{:S(2)}) %collective-permute-start.67) | collective-permute-done | bytes 1179680 | tf_op jit(solution)/shard_map/ppermute | solution.py:363
  432.2 1.6 collective-permute-start.68
  435.8 5.9 %collective-permute-done.79 = bf16[2,2,2,48,1536]{4,3,0,1,2:T(8,128)(2,1)S(1)} collective-permute-done((bf16[2,2,2,48,1536]{4,3,0,1,2:T(8,128)(2,1)S(1)}, bf16[2,2,2,48,1536]{4,3,0,1,2:T(8,128)(2,1)S(1)}, u32[]{:S(2)}, u32[]{:S(2)}) %collective-permute-start.79) | collective-permute-done | bytes 1179680 | tf_op jit(solution)/shard_map/ppermute | solution.py:363
  443.7 10.7 %collective-permute-done.74 = bf16[2,2,48,1536]{3,2,0,1:T(8,128)(2,1)S(1)} collective-permute-done((bf16[2,2,48,1536]{3,2,0,1:T(8,128)(2,1)S(1)}, bf16[2,2,48,1536]{3,2,0,1:T(8,128)(2,1)S(1)}, u32[]{:S(2)}, u32[]{:S(2)}) %collective-permute-start.74) | collective-permute-done | bytes 589856 | tf_op jit(solution)/shard_map/ppermute | solution.py:363
  454.6 10.8 %collective-permute-done.68 = bf16[2,2,48,1536]{3,2,0,1:T(8,128)(2,1)S(1)} collective-permute-done((bf16[2,2,48,1536]{3,2,0,1:T(8,128)(2,1)S(1)}, bf16[2,2,48,1536]{3,2,0,1:T(8,128)(2,1)S(1)}, u32[]{:S(2)}, u32[]{:S(2)}) %collective-permute-start.68) | collective-permute-done | bytes 589856 | tf_op jit(solution)/shard_map/ppermute | solution.py:363
  466.0 2.1 collective-permute-start.87
  468.4 2.5 collective-permute-start.76
  471.0 9.4 %collective-permute-done.69 = bf16[2,48,1536]{2,1,0:T(8,128)(2,1)S(1)} collective-permute-done((bf16[2,48,1536]{2,1,0:T(8,128)(2,1)S(1)}, bf16[2,48,1536]{2,1,0:T(8,128)(2,1)S(1)}, u32[]{:S(2)}, u32[]{:S(2)}) %collective-permute-start.69) | collective-permute-done | bytes 294944 | tf_op jit(solution)/shard_map/ppermute | solution.py:363
  480.6 7.7 %collective-permute-done.87 = bf16[2,48,1536]{2,1,0:T(8,128)(2,1)S(1)} collective-permute-done((bf16[2,48,1536]{2,1,0:T(8,128)(2,1)S(1)}, bf16[2,48,1536]{2,1,0:T(8,128)(2,1)S(1)}, u32[]{:S(2)}, u32[]{:S(2)}) %collective-permute-start.87) | collective-permute-done | bytes 294944 | tf_op jit(solution)/shard_map/ppermute | solution.py:363
  488.5 3.8 collective-permute-done.81
  492.6 7.4 %collective-permute-done.70 = bf16[48,1536]{1,0:T(8,128)(2,1)S(1)} collective-permute-done((bf16[48,1536]{1,0:T(8,128)(2,1)S(1)}, bf16[48,1536]{1,0:T(8,128)(2,1)S(1)}, u32[]{:S(2)}, u32[]{:S(2)}) %collective-permute-start.70) | collective-permute-done | bytes 147488 | tf_op jit(solution)/shard_map/ppermute | solution.py:363
  500.0 3.1 collective-permute-done.88
  (502 shorter events, 137.4 us)
Async XLA Ops:
  0.7 39.8 %collective-permute-start.6 = (bf16[2,768,1536]{2,1,0:T(8,128)(2,1)}, bf16[2,768,1536]{2,1,0:T(8,128)(2,1)}, u32[]{:S(2)}, u32[]{:S(2)}) collective-permute-start(bf16[2,768,1536]{2,1,0:T(8,128)(2,1)} %wuo.7), channel_id=1, source_target_pairs={{0,1},{1,0},{2,3},{3,2},{4,5},{5,4},{6,7},{7,6},{8,9},{9,8},{10,11... | collective-permute-start | bytes 14155784 | tf_op jit(solution)/shard_map/ppermute | solution.py:359
  1.2 39.3 %collective-permute-start.7 = (bf16[2,768,1536]{2,1,0:T(8,128)(2,1)}, bf16[2,768,1536]{2,1,0:T(8,128)(2,1)}, u32[]{:S(2)}, u32[]{:S(2)}) collective-permute-start(bf16[2,768,1536]{2,1,0:T(8,128)(2,1)} %wdo.7), channel_id=1, source_target_pairs={{0,1},{1,0},{2,3},{3,2},{4,5},{5,4},{6,7},{7,6},{8,9},{9,8},{10,11... | collective-permute-start | bytes 14155784 | tf_op jit(solution)/shard_map/ppermute | solution.py:359
  3.3 13.9 %collective-permute-start = (bf16[256,768]{1,0:T(8,128)(2,1)}, bf16[256,768]{1,0:T(8,128)(2,1)S(1)}, u32[]{:S(2)}, u32[]{:S(2)}) collective-permute-start(bf16[256,768]{1,0:T(8,128)(2,1)} %get-tuple-element.192), channel_id=1, source_target_pairs={{0,1},{1,0},{2,3},{3,2},{4,5},{5,4},{6,7},{7,6},{8,9},{9,8},{10,11... | collective-permute-start | bytes 1179656 | tf_op jit(solution)/shard_map/ppermute | solution.py:359
  3.8 15.2 %collective-permute-start.1 = (bf16[2,768,384]{2,1,0:T(8,128)(2,1)S(1)}, bf16[2,768,384]{2,1,0:T(8,128)(2,1)S(1)}, u32[]{:S(2)}, u32[]{:S(2)}) collective-permute-start(bf16[2,768,384]{2,1,0:T(8,128)(2,1)S(1)} %copy-done.4), channel_id=1, source_target_pairs={{0,1},{1,0},{2,3},{3,2},{4,5},{5,4},{6,7},{7,6},{8,9},{9,8},{10,11... | collective-permute-start | bytes 3538952 | tf_op jit(solution)/shard_map/ppermute | solution.py:359
  3.9 8.8 %collective-permute-start.4 = (bf16[2,2304]{1,0:T(2,128)(2,1)S(1)}, bf16[2,2304]{1,0:T(2,128)(2,1)S(1)}, u32[]{:S(2)}, u32[]{:S(2)}) collective-permute-start(bf16[2,2304]{1,0:T(2,128)(2,1)S(1)} %constant_dynamic-update-slice_fusion), channel_id=1, source_target_pairs={{0,1},{1,0},{2,3},{3,2},{4,5},{5,4},{6,7},{7,6},{8,9},{9,8},{10,11... | collective-permute-start | bytes 27656 | tf_op jit(solution)/shard_map/ppermute | solution.py:359
  12.7 5.8 %collective-permute-start.9 = (bf16[256,768]{1,0:T(8,128)(2,1)}, bf16[256,768]{1,0:T(8,128)(2,1)S(1)}, u32[]{:S(2)}, u32[]{:S(2)}) collective-permute-start(bf16[256,768]{1,0:T(8,128)(2,1)} %get-tuple-element.190), channel_id=1, source_target_pairs={{0,1},{1,0},{2,3},{3,2},{4,5},{5,4},{6,7},{7,6},{8,9},{9,8},{10,11... | collective-permute-start | bytes 1179656 | tf_op jit(solution)/shard_map/ppermute | solution.py:359
  18.9 20.6 %collective-permute-start.5 = (bf16[2,768,384]{2,1,0:T(8,128)(2,1)}, bf16[2,768,384]{2,1,0:T(8,128)(2,1)S(1)}, u32[]{:S(2)}, u32[]{:S(2)}) collective-permute-start(bf16[2,768,384]{2,1,0:T(8,128)(2,1)} %woo.7), channel_id=1, source_target_pairs={{0,1},{1,0},{2,3},{3,2},{4,5},{5,4},{6,7},{7,6},{8,9},{9,8},{10,11... | collective-permute-start | bytes 3538952 | tf_op jit(solution)/shard_map/ppermute | solution.py:359
  20.6 176.9 %collective-permute-start.11 = (bf16[512,768]{1,0:T(8,128)(2,1)S(1)}, bf16[512,768]{1,0:T(8,128)(2,1)S(1)}, u32[]{:S(2)}, u32[]{:S(2)}) collective-permute-start(bf16[512,768]{1,0:T(8,128)(2,1)S(1)} %pad_maximum_fusion.x), channel_id=1, source_target_pairs={{0,1},{1,0},{2,3},{3,2},{4,5},{5,4},{6,7},{7,6},{8,9},{9,8},{10,11... | collective-permute-start | bytes 2359304 | tf_op jit(solution)/shard_map/ppermute | solution.py:359
  131.6 40.4 %collective-permute-start.28 = (f32[1,6912]{1,0:T(1,128)S(1)}, f32[1,6912]{1,0:T(1,128)S(1)}, u32[]{:S(2)}, u32[]{:S(2)}) collective-permute-start(f32[1,6912]{1,0:T(1,128)S(1)} %get-tuple-element.217), channel_id=1, source_target_pairs={{0,1},{1,0},{2,3},{3,2},{4,5},{5,4},{6,7},{7,6},{8,9},{9,8},{10,11... | collective-permute-start | bytes 82952 | tf_op jit(solution)/shard_map/ppermute | solution.py:359
  172.1 4.7 collective-permute-start.29
  183.0 5.5 %collective-permute-start.26 = (f32[1,6912]{1,0:T(1,128)S(1)}, f32[1,6912]{1,0:T(1,128)S(1)}, u32[]{:S(2)}, u32[]{:S(2)}) collective-permute-start(f32[1,6912]{1,0:T(1,128)S(1)} %add.416), channel_id=1, source_target_pairs={{0,8},{2,10},{4,12},{6,14},{8,0},{10,2},{12,4},{14,6},{16,24},{18,... | collective-permute-start | bytes 82952 | tf_op jit(solution)/shard_map/ppermute | solution.py:363
  185.6 7.8 %collective-permute-start.32 = (f32[1,6912]{1,0:T(1,128)}, f32[1,6912]{1,0:T(1,128)}, u32[]{:S(2)}, u32[]{:S(2)}) collective-permute-start(f32[1,6912]{1,0:T(1,128)} %add.422), channel_id=1, source_target_pairs={{0,16},{2,18},{4,20},{6,22},{8,24},{10,26},{12,28},{14,30},{16,0},... | collective-permute-start | bytes 82952 | tf_op jit(solution)/shard_map/ppermute | solution.py:363
  189.1 5.2 %collective-permute-start.27 = (f32[1,6912]{1,0:T(1,128)}, f32[1,6912]{1,0:T(1,128)}, u32[]{:S(2)}, u32[]{:S(2)}) collective-permute-start(f32[1,6912]{1,0:T(1,128)} %add.417), channel_id=1, source_target_pairs={{0,16},{2,18},{4,20},{6,22},{8,24},{10,26},{12,28},{14,30},{16,0},... | collective-permute-start | bytes 82952 | tf_op jit(solution)/shard_map/ppermute | solution.py:363
  190.2 43.0 %collective-permute-start.54 = (bf16[512,384]{1,0:T(8,128)(2,1)S(1)}, bf16[512,384]{1,0:T(8,128)(2,1)S(1)}, u32[]{:S(2)}, u32[]{:S(2)}) collective-permute-start(bf16[512,384]{1,0:T(8,128)(2,1)S(1)} %copy-done.20), channel_id=1, source_target_pairs={{0,1},{1,0},{2,3},{3,2},{4,5},{5,4},{6,7},{7,6},{8,9},{9,8},{10,11... | collective-permute-start | bytes 1179656 | tf_op jit(solution)/shard_map/ppermute | solution.py:359
  190.2 36.2 %collective-permute-start.17 = (bf16[512,768]{1,0:T(8,128)(2,1)S(1)}, bf16[512,768]{1,0:T(8,128)(2,1)S(1)}, u32[]{:S(2)}, u32[]{:S(2)}) collective-permute-start(bf16[512,768]{1,0:T(8,128)(2,1)S(1)} %copy-done.3), channel_id=1, source_target_pairs={{0,1},{1,0},{2,3},{3,2},{4,5},{5,4},{6,7},{7,6},{8,9},{9,8},{10,11... | collective-permute-start | bytes 2359304 | tf_op jit(solution)/shard_map/ppermute | solution.py:359
  197.5 30.1 %collective-permute-start.59 = (bf16[512,768]{1,0:T(8,128)(2,1)S(1)}, bf16[512,768]{1,0:T(8,128)(2,1)S(1)}, u32[]{:S(2)}, u32[]{:S(2)}) collective-permute-start(bf16[512,768]{1,0:T(8,128)(2,1)S(1)} %copy-done.45), channel_id=1, source_target_pairs={{0,1},{1,0},{2,3},{3,2},{4,5},{5,4},{6,7},{7,6},{8,9},{9,8},{10,11... | collective-permute-start | bytes 2359304 | tf_op jit(solution)/shard_map/ppermute | solution.py:359
  201.8 9.9 %collective-permute-start.13 = (bf16[2,2,2,48,384]{4,3,1,2,0:T(8,128)(2,1)S(1)}, bf16[2,2,2,48,384]{4,3,1,2,0:T(8,128)(2,1)S(1)}, u32[]{:S(2)}, u32[]{:S(2)}) collective-permute-start(bf16[2,2,2,48,384]{4,3,1,2,0:T(8,128)(2,1)S(1)} %bitcast.414), channel_id=1, source_target_pairs={{0,8},{2,10},{4,12},{6,14},{8,0},{10,2},{12,4},{14,6},{16,24},{18,... | collective-permute-start | bytes 884744 | tf_op jit(solution)/shard_map/ppermute | solution.py:363
  203.6 13.7 %collective-permute-start.34 = (bf16[2,2,2,48,384]{4,3,2,1,0:T(8,128)(2,1)S(1)}, bf16[2,2,2,48,384]{4,3,2,1,0:T(8,128)(2,1)S(1)}, u32[]{:S(2)}, u32[]{:S(2)}) collective-permute-start(bf16[2,2,2,48,384]{4,3,2,1,0:T(8,128)(2,1)S(1)} %dynamic-slice_bitcast_fusion.13), channel_id=1, source_target_pairs={{0,8},{2,10},{4,12},{6,14},{8,0},{10,2},{12,4},{14,6},{16,24},{18,... | collective-permute-start | bytes 884744 | tf_op jit(solution)/shard_map/ppermute | solution.py:363
  211.7 14.1 %collective-permute-start.18 = (bf16[512,384]{1,0:T(8,128)(2,1)S(1)}, bf16[512,384]{1,0:T(8,128)(2,1)S(1)}, u32[]{:S(2)}, u32[]{:S(2)}) collective-permute-start(bf16[512,384]{1,0:T(8,128)(2,1)S(1)} %copy-done.79), channel_id=1, source_target_pairs={{0,1},{1,0},{2,3},{3,2},{4,5},{5,4},{6,7},{7,6},{8,9},{9,8},{10,11... | collective-permute-start | bytes 1179656 | tf_op jit(solution)/shard_map/ppermute | solution.py:359
  217.3 8.3 %collective-permute-start.44 = (bf16[2,2,2,48,384]{4,3,0,1,2:T(8,128)(2,1)S(1)}, bf16[2,2,2,48,384]{4,3,0,1,2:T(8,128)(2,1)S(1)}, u32[]{:S(2)}, u32[]{:S(2)}) collective-permute-start(bf16[2,2,2,48,384]{4,3,0,1,2:T(8,128)(2,1)S(1)} %bitcast.415), channel_id=1, source_target_pairs={{0,4},{2,6},{4,0},{6,2},{8,12},{10,14},{12,8},{14,10},{16,20},{18,... | collective-permute-start | bytes 884744 | tf_op jit(solution)/shard_map/ppermute | solution.py:363
  225.8 8.2 %collective-permute-start.53 = (bf16[512,768]{1,0:T(8,128)(2,1)S(1)}, bf16[512,768]{1,0:T(8,128)(2,1)S(1)}, u32[]{:S(2)}, u32[]{:S(2)}) collective-permute-start(bf16[512,768]{1,0:T(8,128)(2,1)S(1)} %copy-done.46), channel_id=1, source_target_pairs={{0,1},{1,0},{2,3},{3,2},{4,5},{5,4},{6,7},{7,6},{8,9},{9,8},{10,11... | collective-permute-start | bytes 2359304 | tf_op jit(solution)/shard_map/ppermute | solution.py:359
  226.4 157.0 %collective-permute-start.83 = (bf16[512,768]{1,0:T(8,128)(2,1)S(1)}, bf16[512,768]{1,0:T(8,128)(2,1)S(1)}, u32[]{:S(2)}, u32[]{:S(2)}) collective-permute-start(bf16[512,768]{1,0:T(8,128)(2,1)S(1)} %copy-done.7), channel_id=1, source_target_pairs={{0,1},{1,0},{2,3},{3,2},{4,5},{5,4},{6,7},{7,6},{8,9},{9,8},{10,11... | collective-permute-start | bytes 2359304 | tf_op jit(solution)/shard_map/ppermute | solution.py:359
  227.4 9.8 %collective-permute-start.38 = (bf16[512,384]{1,0:T(8,128)(2,1)S(1)}, bf16[512,384]{1,0:T(8,128)(2,1)S(1)}, u32[]{:S(2)}, u32[]{:S(2)}) collective-permute-start(bf16[512,384]{1,0:T(8,128)(2,1)S(1)} %copy-done.77), channel_id=1, source_target_pairs={{0,1},{1,0},{2,3},{3,2},{4,5},{5,4},{6,7},{7,6},{8,9},{9,8},{10,11... | collective-permute-start | bytes 1179656 | tf_op jit(solution)/shard_map/ppermute | solution.py:359
  230.8 142.2 %collective-permute-start.71 = (bf16[512,768]{1,0:T(8,128)(2,1)S(1)}, bf16[512,768]{1,0:T(8,128)(2,1)S(1)}, u32[]{:S(2)}, u32[]{:S(2)}) collective-permute-start(bf16[512,768]{1,0:T(8,128)(2,1)S(1)} %copy-done.53), channel_id=1, source_target_pairs={{0,1},{1,0},{2,3},{3,2},{4,5},{5,4},{6,7},{7,6},{8,9},{9,8},{10,11... | collective-permute-start | bytes 2359304 | tf_op jit(solution)/shard_map/ppermute | solution.py:359
  233.7 139.8 %collective-permute-start.72 = (bf16[512,1536]{1,0:T(8,128)(2,1)S(1)}, bf16[512,1536]{1,0:T(8,128)(2,1)S(1)}, u32[]{:S(2)}, u32[]{:S(2)}) collective-permute-start(bf16[512,1536]{1,0:T(8,128)(2,1)S(1)} %copy-done.75), channel_id=1, source_target_pairs={{0,1},{1,0},{2,3},{3,2},{4,5},{5,4},{6,7},{7,6},{8,9},{9,8},{10,11... | collective-permute-start | bytes 4718600 | tf_op jit(solution)/shard_map/ppermute | solution.py:359
  234.1 13.9 %collective-permute-start.14 = (bf16[2,2,48,384]{3,2,0,1:T(8,128)(2,1)S(1)}, bf16[2,2,48,384]{3,2,0,1:T(8,128)(2,1)S(1)}, u32[]{:S(2)}, u32[]{:S(2)}) collective-permute-start(bf16[2,2,48,384]{3,2,0,1:T(8,128)(2,1)S(1)} %dynamic-slice_bitcast_fusion.25), channel_id=1, source_target_pairs={{0,16},{2,18},{4,20},{6,22},{8,24},{10,26},{12,28},{14,30},{16,0},... | collective-permute-start | bytes 442376 | tf_op jit(solution)/shard_map/ppermute | solution.py:363
  237.3 13.1 %collective-permute-start.35 = (bf16[2,2,48,384]{3,2,1,0:T(8,128)(2,1)S(1)}, bf16[2,2,48,384]{3,2,1,0:T(8,128)(2,1)S(1)}, u32[]{:S(2)}, u32[]{:S(2)}) collective-permute-start(bf16[2,2,48,384]{3,2,1,0:T(8,128)(2,1)S(1)} %dynamic-slice_bitcast_fusion.23), channel_id=1, source_target_pairs={{0,16},{2,18},{4,20},{6,22},{8,24},{10,26},{12,28},{14,30},{16,0},... | collective-permute-start | bytes 442376 | tf_op jit(solution)/shard_map/ppermute | solution.py:363
  248.0 5.1 %collective-permute-start.45 = (bf16[2,2,48,384]{3,2,0,1:T(8,128)(2,1)S(1)}, bf16[2,2,48,384]{3,2,0,1:T(8,128)(2,1)S(1)}, u32[]{:S(2)}, u32[]{:S(2)}) collective-permute-start(bf16[2,2,48,384]{3,2,0,1:T(8,128)(2,1)S(1)} %dynamic-slice_bitcast_fusion.21), channel_id=1, source_target_pairs={{0,2},{2,0},{4,6},{6,4},{8,10},{10,8},{12,14},{14,12},{16,18},{18,... | collective-permute-start | bytes 442376 | tf_op jit(solution)/shard_map/ppermute | solution.py:363
  250.3 29.4 %collective-permute-start.39 = (bf16[2,2,2,48,384]{4,3,2,1,0:T(8,128)(2,1)S(1)}, bf16[2,2,2,48,384]{4,3,2,1,0:T(8,128)(2,1)S(1)}, u32[]{:S(2)}, u32[]{:S(2)}) collective-permute-start(bf16[2,2,2,48,384]{4,3,2,1,0:T(8,128)(2,1)S(1)} %dynamic-slice_bitcast_fusion.12), channel_id=1, source_target_pairs={{0,8},{2,10},{4,12},{6,14},{8,0},{10,2},{12,4},{14,6},{16,24},{18,... | collective-permute-start | bytes 884744 | tf_op jit(solution)/shard_map/ppermute | solution.py:363
  253.1 4.4 collective-permute-start.15
  274.1 5.1 %collective-permute-start.47 = (bf16[48,384]{1,0:T(8,128)(2,1)S(1)}, bf16[48,384]{1,0:T(8,128)(2,1)S(1)}, u32[]{:S(2)}, u32[]{:S(2)}) collective-permute-start(bf16[48,384]{1,0:T(8,128)(2,1)S(1)} %dynamic-slice_bitcast_fusion.37), channel_id=1, source_target_pairs={{0,16},{2,18},{4,20},{6,22},{8,24},{10,26},{12,28},{14,30},{16,0},... | collective-permute-start | bytes 110600 | tf_op jit(solution)/shard_map/ppermute | solution.py:363
  279.2 6.7 %collective-permute-start.19 = (bf16[2,2,2,48,384]{4,3,1,2,0:T(8,128)(2,1)S(1)}, bf16[2,2,2,48,384]{4,3,1,2,0:T(8,128)(2,1)S(1)}, u32[]{:S(2)}, u32[]{:S(2)}) collective-permute-start(bf16[2,2,2,48,384]{4,3,1,2,0:T(8,128)(2,1)S(1)} %bitcast.413), channel_id=1, source_target_pairs={{0,8},{2,10},{4,12},{6,14},{8,0},{10,2},{12,4},{14,6},{16,24},{18,... | collective-permute-start | bytes 884744 | tf_op jit(solution)/shard_map/ppermute | solution.py:363
  279.7 7.9 %collective-permute-start.49 = (bf16[2,2,2,48,384]{4,3,0,1,2:T(8,128)(2,1)S(1)}, bf16[2,2,2,48,384]{4,3,0,1,2:T(8,128)(2,1)S(1)}, u32[]{:S(2)}, u32[]{:S(2)}) collective-permute-start(bf16[2,2,2,48,384]{4,3,0,1,2:T(8,128)(2,1)S(1)} %bitcast.412), channel_id=1, source_target_pairs={{0,4},{2,6},{4,0},{6,2},{8,12},{10,14},{12,8},{14,10},{16,20},{18,... | collective-permute-start | bytes 884744 | tf_op jit(solution)/shard_map/ppermute | solution.py:363
  286.0 6.7 %collective-permute-start.61 = (bf16[2,2,2,48,384]{4,3,0,1,2:T(8,128)(2,1)S(1)}, bf16[2,2,2,48,384]{4,3,0,1,2:T(8,128)(2,1)S(1)}, u32[]{:S(2)}, u32[]{:S(2)}) collective-permute-start(bf16[2,2,2,48,384]{4,3,0,1,2:T(8,128)(2,1)S(1)} %bitcast.411), channel_id=1, source_target_pairs={{0,2},{2,0},{4,6},{6,4},{8,10},{10,8},{12,14},{14,12},{16,18},{18,... | collective-permute-start | bytes 884744 | tf_op jit(solution)/shard_map/ppermute | solution.py:363
  287.6 8.2 %collective-permute-start.55 = (bf16[2,2,2,48,384]{4,3,0,1,2:T(8,128)(2,1)S(1)}, bf16[2,2,2,48,384]{4,3,0,1,2:T(8,128)(2,1)S(1)}, u32[]{:S(2)}, u32[]{:S(2)}) collective-permute-start(bf16[2,2,2,48,384]{4,3,0,1,2:T(8,128)(2,1)S(1)} %bitcast.410), channel_id=1, source_target_pairs={{0,2},{2,0},{4,6},{6,4},{8,10},{10,8},{12,14},{14,12},{16,18},{18,... | collective-permute-start | bytes 884744 | tf_op jit(solution)/shard_map/ppermute | solution.py:363
  292.7 85.9 %collective-permute-start.66 = (bf16[512,1536]{1,0:T(8,128)(2,1)S(1)}, bf16[512,1536]{1,0:T(8,128)(2,1)S(1)}, u32[]{:S(2)}, u32[]{:S(2)}) collective-permute-start(bf16[512,1536]{1,0:T(8,128)(2,1)S(1)} %copy-done.76), channel_id=1, source_target_pairs={{0,1},{1,0},{2,3},{3,2},{4,5},{5,4},{6,7},{7,6},{8,9},{9,8},{10,11... | collective-permute-start | bytes 4718600 | tf_op jit(solution)/shard_map/ppermute | solution.py:359
  295.8 9.8 %collective-permute-start.20 = (bf16[2,2,48,384]{3,2,0,1:T(8,128)(2,1)S(1)}, bf16[2,2,48,384]{3,2,0,1:T(8,128)(2,1)S(1)}, u32[]{:S(2)}, u32[]{:S(2)}) collective-permute-start(bf16[2,2,48,384]{3,2,0,1:T(8,128)(2,1)S(1)} %dynamic-slice_bitcast_fusion.24), channel_id=1, source_target_pairs={{0,16},{2,18},{4,20},{6,22},{8,24},{10,26},{12,28},{14,30},{16,0},... | collective-permute-start | bytes 442376 | tf_op jit(solution)/shard_map/ppermute | solution.py:363
  305.6 6.6 %collective-permute-start.40 = (bf16[2,2,48,384]{3,2,1,0:T(8,128)(2,1)S(1)}, bf16[2,2,48,384]{3,2,1,0:T(8,128)(2,1)S(1)}, u32[]{:S(2)}, u32[]{:S(2)}) collective-permute-start(bf16[2,2,48,384]{3,2,1,0:T(8,128)(2,1)S(1)} %dynamic-slice_bitcast_fusion.22), channel_id=1, source_target_pairs={{0,16},{2,18},{4,20},{6,22},{8,24},{10,26},{12,28},{14,30},{16,0},... | collective-permute-start | bytes 442376 | tf_op jit(solution)/shard_map/ppermute | solution.py:363
  312.2 5.1 %collective-permute-start.50 = (bf16[2,2,48,384]{3,2,0,1:T(8,128)(2,1)S(1)}, bf16[2,2,48,384]{3,2,0,1:T(8,128)(2,1)S(1)}, u32[]{:S(2)}, u32[]{:S(2)}) collective-permute-start(bf16[2,2,48,384]{3,2,0,1:T(8,128)(2,1)S(1)} %dynamic-slice_bitcast_fusion.20), channel_id=1, source_target_pairs={{0,2},{2,0},{4,6},{6,4},{8,10},{10,8},{12,14},{14,12},{16,18},{18,... | collective-permute-start | bytes 442376 | tf_op jit(solution)/shard_map/ppermute | solution.py:363
  317.4 5.1 %collective-permute-start.62 = (bf16[2,2,48,384]{3,2,0,1:T(8,128)(2,1)S(1)}, bf16[2,2,48,384]{3,2,0,1:T(8,128)(2,1)S(1)}, u32[]{:S(2)}, u32[]{:S(2)}) collective-permute-start(bf16[2,2,48,384]{3,2,0,1:T(8,128)(2,1)S(1)} %dynamic-slice_bitcast_fusion.18), channel_id=1, source_target_pairs={{0,4},{2,6},{4,0},{6,2},{8,12},{10,14},{12,8},{14,10},{16,20},{18,... | collective-permute-start | bytes 442376 | tf_op jit(solution)/shard_map/ppermute | solution.py:363
  322.5 5.1 %collective-permute-start.56 = (bf16[2,2,48,384]{3,2,0,1:T(8,128)(2,1)S(1)}, bf16[2,2,48,384]{3,2,0,1:T(8,128)(2,1)S(1)}, u32[]{:S(2)}, u32[]{:S(2)}) collective-permute-start(bf16[2,2,48,384]{3,2,0,1:T(8,128)(2,1)S(1)} %dynamic-slice_bitcast_fusion.19), channel_id=1, source_target_pairs={{0,4},{2,6},{4,0},{6,2},{8,12},{10,14},{12,8},{14,10},{16,20},{18,... | collective-permute-start | bytes 442376 | tf_op jit(solution)/shard_map/ppermute | solution.py:363
  340.7 4.7 collective-permute-start.63
  357.7 4.9 collective-permute-start.52
  362.6 4.9 collective-permute-start.64
  367.5 4.9 collective-permute-start.58
  372.3 16.8 %collective-permute-start.77 = (bf16[512,768]{1,0:T(8,128)(2,1)S(1)}, bf16[512,768]{1,0:T(8,128)(2,1)S(1)}, u32[]{:S(2)}, u32[]{:S(2)}) collective-permute-start(bf16[512,768]{1,0:T(8,128)(2,1)S(1)} %copy-done.9), channel_id=1, source_target_pairs={{0,1},{1,0},{2,3},{3,2},{4,5},{5,4},{6,7},{7,6},{8,9},{9,8},{10,11... | collective-permute-start | bytes 2359304 | tf_op jit(solution)/shard_map/ppermute | solution.py:359
  373.5 10.4 %collective-permute-start.84 = (bf16[512,1536]{1,0:T(8,128)(2,1)S(1)}, bf16[512,1536]{1,0:T(8,128)(2,1)S(1)}, u32[]{:S(2)}, u32[]{:S(2)}) collective-permute-start(bf16[512,1536]{1,0:T(8,128)(2,1)S(1)} %copy-done.74), channel_id=1, source_target_pairs={{0,1},{1,0},{2,3},{3,2},{4,5},{5,4},{6,7},{7,6},{8,9},{9,8},{10,11... | collective-permute-start | bytes 4718600 | tf_op jit(solution)/shard_map/ppermute | solution.py:359
  378.2 10.9 %collective-permute-start.78 = (bf16[512,1536]{1,0:T(8,128)(2,1)S(1)}, bf16[512,1536]{1,0:T(8,128)(2,1)S(1)}, u32[]{:S(2)}, u32[]{:S(2)}) collective-permute-start(bf16[512,1536]{1,0:T(8,128)(2,1)S(1)} %copy-done.73), channel_id=1, source_target_pairs={{0,1},{1,0},{2,3},{3,2},{4,5},{5,4},{6,7},{7,6},{8,9},{9,8},{10,11... | collective-permute-start | bytes 4718600 | tf_op jit(solution)/shard_map/ppermute | solution.py:359
  378.6 28.8 %collective-permute-start.73 = (bf16[2,2,2,48,1536]{4,3,0,1,2:T(8,128)(2,1)S(1)}, bf16[2,2,2,48,1536]{4,3,0,1,2:T(8,128)(2,1)S(1)}, u32[]{:S(2)}, u32[]{:S(2)}) collective-permute-start(bf16[2,2,2,48,1536]{4,3,0,1,2:T(8,128)(2,1)S(1)} %bitcast.402), channel_id=1, source_target_pairs={{0,4},{2,6},{4,0},{6,2},{8,12},{10,14},{12,8},{14,10},{16,20},{18,... | collective-permute-start | bytes 3538952 | tf_op jit(solution)/shard_map/ppermute | solution.py:363
  383.4 48.5 %collective-permute-start.67 = (bf16[2,2,2,48,1536]{4,3,0,1,2:T(8,128)(2,1)S(1)}, bf16[2,2,2,48,1536]{4,3,0,1,2:T(8,128)(2,1)S(1)}, u32[]{:S(2)}, u32[]{:S(2)}) collective-permute-start(bf16[2,2,2,48,1536]{4,3,0,1,2:T(8,128)(2,1)S(1)} %bitcast.403), channel_id=1, source_target_pairs={{0,4},{2,6},{4,0},{6,2},{8,12},{10,14},{12,8},{14,10},{16,20},{18,... | collective-permute-start | bytes 3538952 | tf_op jit(solution)/shard_map/ppermute | solution.py:363
  387.5 46.4 %collective-permute-start.85 = (bf16[2,2,2,48,1536]{4,3,0,1,2:T(8,128)(2,1)S(1)}, bf16[2,2,2,48,1536]{4,3,0,1,2:T(8,128)(2,1)S(1)}, u32[]{:S(2)}, u32[]{:S(2)}) collective-permute-start(bf16[2,2,2,48,1536]{4,3,0,1,2:T(8,128)(2,1)S(1)} %bitcast.404), channel_id=1, source_target_pairs={{0,2},{2,0},{4,6},{6,4},{8,10},{10,8},{12,14},{14,12},{16,18},{18,... | collective-permute-start | bytes 3538952 | tf_op jit(solution)/shard_map/ppermute | solution.py:363
  392.3 49.4 %collective-permute-start.79 = (bf16[2,2,2,48,1536]{4,3,0,1,2:T(8,128)(2,1)S(1)}, bf16[2,2,2,48,1536]{4,3,0,1,2:T(8,128)(2,1)S(1)}, u32[]{:S(2)}, u32[]{:S(2)}) collective-permute-start(bf16[2,2,2,48,1536]{4,3,0,1,2:T(8,128)(2,1)S(1)} %bitcast.405), channel_id=1, source_target_pairs={{0,2},{2,0},{4,6},{6,4},{8,10},{10,8},{12,14},{14,12},{16,18},{18,... | collective-permute-start | bytes 3538952 | tf_op jit(solution)/shard_map/ppermute | solution.py:363
  407.8 46.5 %collective-permute-start.74 = (bf16[2,2,48,1536]{3,2,0,1:T(8,128)(2,1)S(1)}, bf16[2,2,48,1536]{3,2,0,1:T(8,128)(2,1)S(1)}, u32[]{:S(2)}, u32[]{:S(2)}) collective-permute-start(bf16[2,2,48,1536]{3,2,0,1:T(8,128)(2,1)S(1)} %dynamic-slice_bitcast_fusion.2), channel_id=1, source_target_pairs={{0,2},{2,0},{4,6},{6,4},{8,10},{10,8},{12,14},{14,12},{16,18},{18,... | collective-permute-start | bytes 1769480 | tf_op jit(solution)/shard_map/ppermute | solution.py:363
  432.2 33.2 %collective-permute-start.68 = (bf16[2,2,48,1536]{3,2,0,1:T(8,128)(2,1)S(1)}, bf16[2,2,48,1536]{3,2,0,1:T(8,128)(2,1)S(1)}, u32[]{:S(2)}, u32[]{:S(2)}) collective-permute-start(bf16[2,2,48,1536]{3,2,0,1:T(8,128)(2,1)S(1)} %dynamic-slice_bitcast_fusion.3), channel_id=1, source_target_pairs={{0,2},{2,0},{4,6},{6,4},{8,10},{10,8},{12,14},{14,12},{16,18},{18,... | collective-permute-start | bytes 1769480 | tf_op jit(solution)/shard_map/ppermute | solution.py:363
  434.2 31.5 %collective-permute-start.86 = (bf16[2,2,48,1536]{3,2,0,1:T(8,128)(2,1)S(1)}, bf16[2,2,48,1536]{3,2,0,1:T(8,128)(2,1)S(1)}, u32[]{:S(2)}, u32[]{:S(2)}) collective-permute-start(bf16[2,2,48,1536]{3,2,0,1:T(8,128)(2,1)S(1)} %dynamic-slice_bitcast_fusion), channel_id=1, source_target_pairs={{0,4},{2,6},{4,0},{6,2},{8,12},{10,14},{12,8},{14,10},{16,20},{18,... | collective-permute-start | bytes 1769480 | tf_op jit(solution)/shard_map/ppermute | solution.py:363
  442.1 26.0 %collective-permute-start.80 = (bf16[2,2,48,1536]{3,2,0,1:T(8,128)(2,1)S(1)}, bf16[2,2,48,1536]{3,2,0,1:T(8,128)(2,1)S(1)}, u32[]{:S(2)}, u32[]{:S(2)}) collective-permute-start(bf16[2,2,48,1536]{3,2,0,1:T(8,128)(2,1)S(1)} %dynamic-slice_bitcast_fusion.1), channel_id=1, source_target_pairs={{0,4},{2,6},{4,0},{6,2},{8,12},{10,14},{12,8},{14,10},{16,20},{18,... | collective-permute-start | bytes 1769480 | tf_op jit(solution)/shard_map/ppermute | solution.py:363
  454.6 13.8 %collective-permute-start.75 = (bf16[2,48,1536]{2,1,0:T(8,128)(2,1)S(1)}, bf16[2,48,1536]{2,1,0:T(8,128)(2,1)S(1)}, u32[]{:S(2)}, u32[]{:S(2)}) collective-permute-start(bf16[2,48,1536]{2,1,0:T(8,128)(2,1)S(1)} %dynamic-slice_bitcast_fusion.10), channel_id=1, source_target_pairs={{0,8},{2,10},{4,12},{6,14},{8,0},{10,2},{12,4},{14,6},{16,24},{18,... | collective-permute-start | bytes 884744 | tf_op jit(solution)/shard_map/ppermute | solution.py:363
  465.7 14.8 %collective-permute-start.69 = (bf16[2,48,1536]{2,1,0:T(8,128)(2,1)S(1)}, bf16[2,48,1536]{2,1,0:T(8,128)(2,1)S(1)}, u32[]{:S(2)}, u32[]{:S(2)}) collective-permute-start(bf16[2,48,1536]{2,1,0:T(8,128)(2,1)S(1)} %dynamic-slice_bitcast_fusion.11), channel_id=1, source_target_pairs={{0,8},{2,10},{4,12},{6,14},{8,0},{10,2},{12,4},{14,6},{16,24},{18,... | collective-permute-start | bytes 884744 | tf_op jit(solution)/shard_map/ppermute | solution.py:363
  466.0 22.4 %collective-permute-start.87 = (bf16[2,48,1536]{2,1,0:T(8,128)(2,1)S(1)}, bf16[2,48,1536]{2,1,0:T(8,128)(2,1)S(1)}, u32[]{:S(2)}, u32[]{:S(2)}) collective-permute-start(bf16[2,48,1536]{2,1,0:T(8,128)(2,1)S(1)} %dynamic-slice_bitcast_fusion.8), channel_id=1, source_target_pairs={{0,8},{2,10},{4,12},{6,14},{8,0},{10,2},{12,4},{14,6},{16,24},{18,... | collective-permute-start | bytes 884744 | tf_op jit(solution)/shard_map/ppermute | solution.py:363
  468.2 24.1 %collective-permute-start.81 = (bf16[2,48,1536]{2,1,0:T(8,128)(2,1)S(1)}, bf16[2,48,1536]{2,1,0:T(8,128)(2,1)S(1)}, u32[]{:S(2)}, u32[]{:S(2)}) collective-permute-start(bf16[2,48,1536]{2,1,0:T(8,128)(2,1)S(1)} %dynamic-slice_bitcast_fusion.9), channel_id=1, source_target_pairs={{0,8},{2,10},{4,12},{6,14},{8,0},{10,2},{12,4},{14,6},{16,24},{18,... | collective-permute-start | bytes 884744 | tf_op jit(solution)/shard_map/ppermute | solution.py:363
  468.4 24.1 %collective-permute-start.76 = (bf16[48,1536]{1,0:T(8,128)(2,1)S(1)}, bf16[48,1536]{1,0:T(8,128)(2,1)S(1)}, u32[]{:S(2)}, u32[]{:S(2)}) collective-permute-start(bf16[48,1536]{1,0:T(8,128)(2,1)S(1)} %dynamic-slice_bitcast_fusion.16), channel_id=1, source_target_pairs={{0,16},{2,18},{4,20},{6,22},{8,24},{10,26},{12,28},{14,30},{16,0},... | collective-permute-start | bytes 442376 | tf_op jit(solution)/shard_map/ppermute | solution.py:363
  480.5 19.5 %collective-permute-start.70 = (bf16[48,1536]{1,0:T(8,128)(2,1)S(1)}, bf16[48,1536]{1,0:T(8,128)(2,1)S(1)}, u32[]{:S(2)}, u32[]{:S(2)}) collective-permute-start(bf16[48,1536]{1,0:T(8,128)(2,1)S(1)} %dynamic-slice_bitcast_fusion.17), channel_id=1, source_target_pairs={{0,16},{2,18},{4,20},{6,22},{8,24},{10,26},{12,28},{14,30},{16,0},... | collective-permute-start | bytes 442376 | tf_op jit(solution)/shard_map/ppermute | solution.py:363
  488.4 14.7 %collective-permute-start.88 = (bf16[48,1536]{1,0:T(8,128)(2,1)S(1)}, bf16[48,1536]{1,0:T(8,128)(2,1)S(1)}, u32[]{:S(2)}, u32[]{:S(2)}) collective-permute-start(bf16[48,1536]{1,0:T(8,128)(2,1)S(1)} %dynamic-slice_bitcast_fusion.14), channel_id=1, source_target_pairs={{0,16},{2,18},{4,20},{6,22},{8,24},{10,26},{12,28},{14,30},{16,0},... | collective-permute-start | bytes 442376 | tf_op jit(solution)/shard_map/ppermute | solution.py:363
  492.4 12.6 %collective-permute-start.82 = (bf16[48,1536]{1,0:T(8,128)(2,1)S(1)}, bf16[48,1536]{1,0:T(8,128)(2,1)S(1)}, u32[]{:S(2)}, u32[]{:S(2)}) collective-permute-start(bf16[48,1536]{1,0:T(8,128)(2,1)S(1)} %dynamic-slice_bitcast_fusion.15), channel_id=1, source_target_pairs={{0,16},{2,18},{4,20},{6,22},{8,24},{10,26},{12,28},{14,30},{16,0},... | collective-permute-start | bytes 442376 | tf_op jit(solution)/shard_map/ppermute | solution.py:363
  (111 other events, 713.1 us)
